TPU v7x, 256 devices: a whole 4x4x8 slice. The times are simulated.
256 devices in a mesh: narrow: 8 (over y, z_lo), wide: 8 (over z_hi, core), nys: 4 (over x).
Axes of the slice: x: 4, y: 4, z: 8 (z_hi: 4, z_lo: 2; z = z_hi * 2 + z_lo), core: 2. Of those that a mesh axis runs over, the one named last changes fastest.
Arguments:
- centers: bfloat16 [262144, 1024], P(('narrow', 'wide', 'nys')), may hold values from -6 to 6
- weights: float32 [262144, 1000], P(('narrow', 'wide', 'nys')), may hold values from -6 to 6
- batch_points: bfloat16 [512, 1024], P(('narrow', 'wide', 'nys')), may hold values from -6 to 6
- labels: float32 [512, 1000], P(('narrow', 'wide', 'nys')), may hold values from -6 to 6
- nystrom_points: bfloat16 [2048, 1024], P(('narrow', 'nys')), may hold values from -6 to 6
- eigvecs: float32 [2048, 160], P(('narrow', 'nys')), may hold values from -0.125 to 0.125
- corrections: float32 [160], replicated, may hold values from 0.05 to 0.5
Outputs:
- new_weights: float32 [262144, 1000], P(('narrow', 'wide', 'nys'))
All inputs are finite; a program needn't handle non-finite values.
Results may differ from a plain program's by a relative error of at most 0.0003.
The roundings to bfloat16 on the way count: a program that leaves them out, or rounds other values in their place, can miss the bound.
Values may be sent and summed in bfloat16 or wider, within the bound.
A program may use at most 64 MiB of HBM per device.

v0:
```python
import math

import jax
import jax.numpy as jnp
from jax import lax
from jax.sharding import PartitionSpec as P

BATCH = 512


RATE = 16.0
SPREAD = 4.0


def kernel_with(left, left_sq, right):
    cross = lax.dot_general(
        left, right, (((1,), (1,)), ((), ())), preferred_element_type=jnp.float32
    )
    right_sq = jnp.sum(jnp.square(right.astype(jnp.float32)), axis=1)
    dist = jnp.sqrt(jnp.maximum(left_sq[:, None] + right_sq[None, :] - 2.0 * cross, 0.0))
    radius = math.sqrt(2.0 * left.shape[1])
    return jnp.exp((radius - dist) / SPREAD).astype(jnp.bfloat16)


def squares(points):
    return jnp.sum(jnp.square(points.astype(jnp.float32)), axis=1)


def per_device(centers, weights, batch_points, labels, nystrom_points, eigvecs, corrections):
    batch_all = lax.all_gather(batch_points, ("narrow", "wide", "nys"), axis=0, tiled=True)
    count = lax.axis_size(("narrow", "wide", "nys"))
    scale = (centers.shape[0] * count) ** (-0.5)
    center_sq = squares(centers)
    k_batch = kernel_with(centers, center_sq, batch_all)
    partial_value = (
        lax.dot_general(
            k_batch,
            weights.astype(jnp.bfloat16),
            (((0,), (0,)), ((), ())),
            preferred_element_type=jnp.float32,
        )
        * scale
    )
    rows = labels.shape[0]
    offset = lax.axis_index(("narrow", "wide", "nys")) * rows
    placed = lax.dynamic_update_slice(jnp.zeros_like(partial_value), labels, (offset, jnp.int32(0)))
    residual = lax.psum(partial_value - placed, ("narrow", "wide", "nys")).astype(jnp.bfloat16)
    k_nystrom = kernel_with(nystrom_points, squares(nystrom_points), batch_all)
    pulled = jnp.dot(k_nystrom, residual, preferred_element_type=jnp.float32)
    local_proj = lax.dot_general(
        eigvecs, pulled, (((0,), (0,)), ((), ())), precision=lax.Precision.HIGHEST
    )
    projected = lax.psum(local_proj, ("narrow", "nys"))
    scaled_proj = corrections[:, None] * projected
    gradient = jnp.dot(k_batch, residual, preferred_element_type=jnp.float32)
    corrected = jnp.dot(eigvecs, scaled_proj, precision=lax.Precision.HIGHEST).astype(jnp.bfloat16)
    points = lax.all_gather(nystrom_points, ("narrow", "nys"), axis=0, tiled=True)
    coefs = lax.all_gather(corrected, ("narrow", "nys"), axis=0, tiled=True)
    tile = kernel_with(centers, center_sq, points)
    nystrom_term = jnp.dot(tile, coefs, preferred_element_type=jnp.float32)
    return weights - RATE / BATCH * (gradient - nystrom_term)


def solution(mesh):
    placed = (
        P(("narrow", "wide", "nys"), None),
        P(("narrow", "wide", "nys"), None),
        P(("narrow", "wide", "nys"), None),
        P(("narrow", "wide", "nys"), None),
        P(("narrow", "nys"), None),
        P(("narrow", "nys"), None),
        P(),
    )
    return jax.shard_map(
        per_device,
        mesh=mesh,
        in_specs=placed,
        out_specs=P(("narrow", "wide", "nys"), None),
        check_vma=False,
    )
```

profile of v0, /device:TPU:1, one launch (start us, length us, event | category | flops | bytes accessed | tf_op | source)
XLA Modules:
  0.0 1267.8 jit_solution(18334620316952581570)
XLA Ops:
  6.5 0.0 copy-start
  6.5 0.0 all-gather.9.cloned.1.call-start
  6.5 0.7 all-gather.9.cloned.1.call-update
  7.3 0.0 all-reduce.3.cloned.1.call-start
  7.3 0.9 copy.9
  8.2 0.2 broadcast_in_dim.2
  8.5 6.3 dynamic_update_slice.3
  14.8 1.0 multiply_reduce_fusion.3
  15.8 2.1 multiply_reduce_fusion.1
  17.9 524.9 %all-gather.9.cloned.1.call-done = bf16[256,2,1024]{2,1,0:T(2,128)(2,1)} async-done(((bf16[1,2,1024]{2,1,0:T(2,128)(2,1)}), bf16[256,2,1024]{2,1,0:T(2,128)(2,1)}) %all-gather.9.cloned.1.call-update) | async-done | bytes 1048592 | tf_op jit(solution)/shard_map/all_gather | solution.py:30
  542.8 1.5 reshape.6
  544.3 0.3 multiply_reduce_fusion.2
  544.6 0.0 copy-start.1
  544.6 3.8 exponential_convert_fusion.1
  548.4 0.0 copy-start.2
  548.4 1.1 copy-done.2
  549.5 0.0 copy-done.1
  549.5 0.0 copy-start.4
  549.5 2.6 multiply_subtract_fusion.1
  552.0 0.0 copy-start.5
  552.0 82.7 %all-reduce.4 = bf16[512,1000]{0,1:T(8,128)(2,1)S(1)} all-reduce(f32[512,1000]{0,1:T(8,128)} %multiply_subtract_fusion.1), channel_id=1, replica_groups=mesh['narrow'=8,'wide'=8,'nys'=4] {'narrow','wide','nys'}, use_global_device_ids=true, to_apply=%region_2.0 | all-reduce | flops 512000 | bytes 3072000 | tf_op jit(solution)/shard_map/psum | solution.py:47
  634.7 0.0 copy-done.4
  634.8 0.8 fusion.12
  635.6 0.0 copy-done
  635.6 1.6 convolution_bitcast_fusion
  637.2 0.0 all-reduce.3.cloned.1.call-update
  637.2 0.0 all-gather.5.cloned.1.call-start
  637.2 0.7 all-gather.5.cloned.1.call-update
  637.9 0.2 all-gather.7.cloned.1.call-start
  638.2 279.8 %all-reduce.3.cloned.1.call-done = f32[160,1000]{1,0:T(8,128)} async-done(((f32[160,1000]{1,0:T(8,128)}), f32[160,1000]{1,0:T(8,128)}) %all-reduce.3.cloned.1.call-update) | async-done | bytes 640016 | tf_op jit(solution)/shard_map/psum | solution.py:53
  918.0 0.0 copy-done.5
  918.0 2.3 fusion.4
  920.3 0.0 all-gather.7.cloned.1.call-update
  920.3 157.8 %all-gather.5.cloned.1.call-done = bf16[2048,1024]{1,0:T(8,128)(2,1)} async-done(((bf16[64,1024]{1,0:T(8,128)(2,1)}), bf16[2048,1024]{1,0:T(8,128)(2,1)}) %all-gather.5.cloned.1.call-update) | async-done | bytes 4194320 | tf_op jit(solution)/shard_map/all_gather | solution.py:57
  1078.2 3.1 multiply_reduce_fusion
  1081.2 0.0 copy-start.3
  1081.2 157.9 %all-gather.7.cloned.1.call-done = bf16[2048,1000]{1,0:T(8,128)(2,1)} async-done(((bf16[64,1000]{1,0:T(8,128)(2,1)}), bf16[2048,1000]{1,0:T(8,128)(2,1)}) %all-gather.7.cloned.1.call-update) | async-done | bytes 4096016 | tf_op jit(solution)/shard_map/all_gather | solution.py:58
  1239.2 15.5 %fusion.13 = f32[1024,1000]{0,1:T(8,128)} fusion(bf16[2048,1000]{1,0:T(8,128)(2,1)} %all-gather.7.cloned.1.call-done, bf16[1024,1024]{1,0:T(8,128)(2,1)} %param.7, bf16[2048,1024]{1,0:T(8,128)(2,1)} %all-gather.5.cloned.1.call-done, f32[2048]{0:T(1024)S(1)} %multiply_reduce_fusion, f32[1024]{0:T(1024)S(1)} %multiply_reduce_fusion.1), kind=kOutput, calls=%fused_computation.21 | convolution fusion | flops 8503951360 | bytes 14495744 | tf_op jit(solution)/shard_map/dot_general | solution.py:60
  1254.6 0.0 copy-done.3
  1254.6 6.7 multiply_subtract_fusion
Async XLA Ops:
  6.5 629.1 %copy-start = (f32[64,160]{1,0:T(8,128)S(1)}, f32[64,160]{1,0:T(8,128)}, u32[]{:S(2)}) copy-start(f32[64,160]{1,0:T(8,128)} %param.12) | copy-start | bytes 122884
  6.5 536.3 %all-gather.9.cloned.1.call-start = ((), (), s32[]{:S(2)}) async-start(), calls=%async_computation.3 | async-start | bytes 1052672 | tf_op jit(solution)/shard_map/all_gather | solution.py:30
  7.3 910.7 %all-reduce.3.cloned.1.call-start = ((), (), s32[]{:S(2)}) async-start(), calls=%async_computation.1 | async-start | bytes 1310720 | tf_op jit(solution)/shard_map/psum | solution.py:53
  544.6 4.9 copy-start.1
  548.4 1.1 copy-start.2
  549.5 85.3 %copy-start.4 = (bf16[64,1024]{1,0:T(8,128)(2,1)S(1)}, bf16[64,1024]{1,0:T(8,128)(2,1)}, u32[]{:S(2)}) copy-start(bf16[64,1024]{1,0:T(8,128)(2,1)} %param.11) | copy-start | bytes 393220
  552.0 365.9 %copy-start.5 = (f32[160]{0:T(256)S(1)}, f32[160]{0:T(256)}, u32[]{:S(2)}) copy-start(f32[160]{0:T(256)} %param.13) | copy-start | bytes 1924
  637.2 441.0 %all-gather.5.cloned.1.call-start = ((), (), s32[]{:S(2)}) async-start(), calls=%async_computation | async-start | bytes 4325376 | tf_op jit(solution)/shard_map/all_gather | solution.py:57
  637.9 601.2 %all-gather.7.cloned.1.call-start = ((), (), s32[]{:S(2)}) async-start(), calls=%async_computation.2 | async-start | bytes 4325376 | tf_op jit(solution)/shard_map/all_gather | solution.py:58
  1081.2 173.4 %copy-start.3 = (bf16[1024,512]{1,0:T(8,128)(2,1)S(1)}, bf16[1024,512]{1,0:T(8,128)(2,1)}, u32[]{:S(2)}) copy-start(bf16[1024,512]{1,0:T(8,128)(2,1)} %copy-done.2) | copy-start | bytes 3145732
Sparse Core Ops, SparseCore 0:
  9.2 533.6 all-gather.8
  637.3 280.5 all-reduce.2
  919.9 158.2 all-gather.4
  1079.9 159.1 all-gather.6
where the time goes:
time: 1290 us; the launch traced here: 1270 us
  waiting for transfers between devices  1120 us (87%)
  blocking collectives  82.7 us (6%)
  matrix products  33.3 us (3%)
  between operations  13.2 us (1%)
    all_gather x1, waiting for transfers between devices, per_device(): lax.all_gather(batch_points, ('narrow', 'wide', 'nys'), axis=0, tiled=True)  525 us
    psum x1, waiting for transfers between devices, per_device(): projected = lax.psum(local_proj, ('narrow', 'nys'))  280 us
    all_gather x1, waiting for transfers between devices, per_device(): coefs = lax.all_gather(corrected, ('narrow', 'nys'), axis=0, tiled=True)  158 us
    all_gather x1, waiting for transfers between devices, per_device(): lax.all_gather(nystrom_points, ('narrow', 'nys'), axis=0, tiled=True)  158 us
    psum x1, blocking collectives, per_device(): lax.psum(partial_value - placed, ('narrow', 'wide', 'nys'))  82.7 us
  transfers between devices with their start and end apart: 4, of which 4 were waited for; matrix products, arithmetic and copies ran while one was open for 1% of the time, Pallas kernels for 0%

commit v1 on v0

v1 whole, which is shorter than its diff:
```python
import functools
import math

import jax
import jax.numpy as jnp
from jax import lax
from jax.experimental import pallas as pl
from jax.experimental.pallas import tpu as pltpu
from jax.sharding import PartitionSpec as P

RATE = 16.0
SPREAD = 4.0
MESH = pl.DeviceIdType.MESH


def place():
    n, w, x = (lax.axis_index(a) for a in ("narrow", "wide", "nys"))
    y, zl = n // 2, n % 2
    zh, c = w // 2, w % 2
    return x, y, zh * 2 + zl, c


def device(x, y, z, c):
    return (y * 2 + z % 2, (z // 2) * 2 + c, x)


class Links:
    def __init__(self):
        self.x, self.y, self.z, self.c = place()
        self.p = self.x * (1 - self.c) + self.y * self.c
        self.q = self.y * (1 - self.c) + self.x * self.c

    def core(self):
        return device(self.x, self.y, self.z, 1 - self.c)

    def along_p(self, k):
        c = self.c
        return device((self.x + k * (1 - c)) % 4, (self.y + k * c) % 4, self.z, c)

    def along_q(self, k):
        c = self.c
        return device((self.x + k * c) % 4, (self.y + k * (1 - c)) % 4, self.z, c)

    def along_z(self, k):
        return device(self.x, self.y, (self.z + k) % 8, self.c)

    def z_pair(self):
        return device(self.x, self.y, self.z + 1 - 2 * (self.z % 2), self.c)

    def greet(self):
        barrier = pltpu.get_barrier_semaphore()
        peers = [self.core()]
        peers += [self.along_p(k) for k in range(1, 4)]
        peers += [self.along_q(k) for k in range(1, 4)]
        peers += [self.along_z(k) for k in range(1, 8)]
        for peer in peers:
            pl.semaphore_signal(barrier, inc=1, device_id=peer, device_id_type=MESH)
        pl.semaphore_wait(barrier, len(peers))


class Copies:
    def __init__(self, send, recv):
        self.send, self.recv, self.next = send, recv, 0

    def start(self, pairs):
        out = []
        for src, dst, peer in pairs:
            copy = pltpu.make_async_remote_copy(
                src_ref=src,
                dst_ref=dst,
                send_sem=self.send.at[self.next],
                recv_sem=self.recv.at[self.next],
                device_id=peer,
                device_id_type=MESH,
            )
            self.next += 1
            copy.start()
            out.append(copy)
        return out


def arrived(copies):
    for copy in copies:
        copy.wait_recv()


def sent(copies):
    for copy in copies:
        copy.wait_send()


def rows(ref, start, size, unit):
    return ref.at[pl.ds(pl.multiple_of(start, unit), size), :]


def gather_tiles(links, copies, ref):
    c, p, q, z = links.c, links.p, links.q, links.z
    tile = ref.at[
        pl.ds(pl.multiple_of(c * 256 + p * 64 + q * 16, 16), 16),
        pl.ds(pl.multiple_of(z * 128, 128), 128),
    ]
    out = copies.start([(tile, tile, links.along_z(k)) for k in range(1, 8)])
    yield out
    arrived(out)
    block = rows(ref, c * 256 + p * 64 + q * 16, 16, 16)
    out = copies.start([(block, block, links.along_q(k)) for k in range(1, 4)])
    yield out
    arrived(out)
    block = rows(ref, c * 256 + p * 64, 64, 64)
    out = copies.start([(block, block, links.along_p(k)) for k in range(1, 4)])
    yield out
    arrived(out)
    block = rows(ref, c * 256, 256, 256)
    out = copies.start([(block, block, links.core())])
    yield out
    arrived(out)
    yield []


def gather_shards(links, copies, refs):
    c, p, q, zl = links.c, links.p, links.q, links.z % 2
    own = [rows(r, c * 1024 + p * 256 + q * 64 + zl * 32, 32, 32) for r in refs]
    out = copies.start([(o, o, links.z_pair()) for o in own])
    yield out
    arrived(out)
    own = [rows(r, c * 1024 + p * 256 + q * 64, 64, 64) for r in refs]
    out = copies.start([(o, o, links.along_q(k)) for k in range(1, 4) for o in own])
    yield out
    arrived(out)
    own = [rows(r, c * 1024 + p * 256, 256, 256) for r in refs]
    out = copies.start([(o, o, links.along_p(k)) for k in range(1, 4) for o in own])
    yield out
    arrived(out)
    own = [rows(r, c * 1024, 1024, 1024) for r in refs]
    out = copies.start([(o, o, links.core()) for o in own])
    yield out
    arrived(out)
    yield []


def gather_kernel(batch, nystrom, eig, batch_all, nystrom_all, eig_all, send, recv):
    links = Links()
    c, p, q, z = links.c, links.p, links.q, links.z
    row, col = c * 256 + p * 64 + q * 16, z * 128
    batch_all[pl.ds(pl.multiple_of(row, 16), 16), pl.ds(pl.multiple_of(col, 128), 128)] = batch[...]
    row = pl.multiple_of(c * 1024 + p * 256 + q * 64 + (z % 2) * 32, 32)
    half = pl.ds(pl.multiple_of(c * 32, 32), 32)
    nystrom_all[pl.ds(row, 32), :] = nystrom[half, :]
    eig_all[pl.ds(row, 32), :] = eig[half, :]
    links.greet()
    copies = Copies(send, recv)
    first = gather_tiles(links, copies, batch_all)
    second = gather_shards(links, copies, (nystrom_all, eig_all))
    started = []
    for _ in range(5):
        started += next(first)
        started += next(second)
    sent(started)


def gather(batch, nystrom, eig):
    vmem = pl.BlockSpec(memory_space=pltpu.VMEM)
    return pl.pallas_call(
        gather_kernel,
        out_shape=(
            jax.ShapeDtypeStruct((512, 1024), jnp.bfloat16),
            jax.ShapeDtypeStruct((2048, 1024), jnp.bfloat16),
            jax.ShapeDtypeStruct((2048, 256), jnp.float32),
        ),
        in_specs=[vmem] * 3,
        out_specs=(vmem,) * 3,
        scratch_shapes=[pltpu.SemaphoreType.DMA((30,)), pltpu.SemaphoreType.DMA((30,))],
        compiler_params=pltpu.CompilerParams(
            collective_id=0, has_side_effects=True, vmem_limit_bytes=40 << 20
        ),
        name="gather",
    )(batch, nystrom, eig)


def add_up(out, terms):
    count = out.shape[0]
    step = min(count, 16)

    def body(i, carry):
        at = pl.ds(pl.multiple_of(i * step, step), step)
        total = terms[0][at, :]
        for term in terms[1:]:
            total = total + term[at, :]
        out[at, :] = total.astype(out.dtype)
        return carry

    lax.fori_loop(0, count // step, body, 0)


def reduce_kernel(part, labels, resid, sum0, sum1, sum2, from_core, from_p, from_q, from_z, send, recv):
    links = Links()
    c, p, q, z = links.c, links.p, links.q, links.z
    group = c * 16 + p * 4 + q
    links.greet()
    copies = Copies(send, recv)
    started = out = copies.start([(rows(part, (1 - c) * 256, 256, 256), from_core, links.core())])
    arrived(out)
    add_up(sum0, [rows(part, c * 256, 256, 256), from_core])
    out = copies.start(
        [
            (rows(sum0, ((p + k) % 4) * 64, 64, 64), from_p.at[k - 1], links.along_p(k))
            for k in range(1, 4)
        ]
    )
    started += out
    arrived(out)
    add_up(sum1, [rows(sum0, p * 64, 64, 64)] + [from_p.at[k] for k in range(3)])
    out = copies.start(
        [
            (rows(sum1, ((q + k) % 4) * 16, 16, 16), from_q.at[k - 1], links.along_q(k))
            for k in range(1, 4)
        ]
    )
    started += out
    arrived(out)
    line = lax.broadcasted_iota(jnp.int32, (16, 1024), 0) - z * 2
    placed = jnp.where(line == 0, labels[0:1, :], jnp.where(line == 1, labels[1:2, :], 0.0))
    total = sum1[pl.ds(pl.multiple_of(q * 16, 16), 16), :] - placed
    for k in range(3):
        total = total + from_q[k]
    sum2[...] = total
    out = copies.start(
        [
            (
                sum2.at[:, pl.ds(pl.multiple_of(((z + k) % 8) * 128, 128), 128)],
                from_z.at[k - 1],
                links.along_z(k),
            )
            for k in range(1, 8)
        ]
    )
    started += out
    arrived(out)
    total = sum2[:, pl.ds(pl.multiple_of(z * 128, 128), 128)]
    for k in range(7):
        total = total + from_z[k]
    resid[
        pl.ds(pl.multiple_of(group * 16, 16), 16), pl.ds(pl.multiple_of(z * 128, 128), 128)
    ] = total.astype(resid.dtype)
    for out in gather_tiles(links, copies, resid):
        started += out
    sent(started)


def reduce(part, labels):
    vmem = pl.BlockSpec(memory_space=pltpu.VMEM)
    return pl.pallas_call(
        reduce_kernel,
        out_shape=jax.ShapeDtypeStruct((512, 1024), jnp.bfloat16),
        in_specs=[vmem] * 2,
        out_specs=vmem,
        scratch_shapes=[
            pltpu.VMEM((256, 1024), jnp.float32),
            pltpu.VMEM((64, 1024), jnp.float32),
            pltpu.VMEM((16, 1024), jnp.float32),
            pltpu.VMEM((256, 1024), jnp.float32),
            pltpu.VMEM((3, 64, 1024), jnp.float32),
            pltpu.VMEM((3, 16, 1024), jnp.float32),
            pltpu.VMEM((7, 16, 128), jnp.float32),
            pltpu.SemaphoreType.DMA((28,)),
            pltpu.SemaphoreType.DMA((28,)),
        ],
        compiler_params=pltpu.CompilerParams(
            collective_id=1, has_side_effects=True, vmem_limit_bytes=40 << 20
        ),
        name="reduce",
    )(part, labels)


def kernel_of(left, left_sq, right, right_sq):
    cross = lax.dot_general(
        left, right, (((1,), (1,)), ((), ())), preferred_element_type=jnp.float32
    )
    dist = jnp.sqrt(jnp.maximum(left_sq[:, None] + right_sq[None, :] - 2.0 * cross, 0.0))
    radius = math.sqrt(2.0 * left.shape[1])
    return jnp.exp((radius - dist) / SPREAD).astype(jnp.bfloat16)


def squares(points):
    return jnp.sum(jnp.square(points.astype(jnp.float32)), axis=1)


def per_device(centers, weights, batch_points, labels, nystrom_points, eigvecs, corrections):
    outs = weights.shape[1]
    scale = (centers.shape[0] * 256) ** (-0.5)
    tiles, points, eig = gather(
        batch_points.reshape(16, 128),
        nystrom_points,
        jnp.pad(eigvecs, ((0, 0), (0, 256 - eigvecs.shape[1]))),
    )
    eig = eig[:, : eigvecs.shape[1]]
    batch = tiles.reshape(32, 2, 8, 8, 128).transpose(0, 3, 1, 2, 4).reshape(512, 1024)
    center_sq, batch_sq, points_sq = squares(centers), squares(batch), squares(points)
    k_batch = kernel_of(centers, center_sq, batch, batch_sq)
    part = (
        lax.dot_general(
            k_batch,
            weights.astype(jnp.bfloat16),
            (((0,), (0,)), ((), ())),
            preferred_element_type=jnp.float32,
        )
        * scale
    )
    wide = ((0, 0), (0, 1024 - outs))
    resid = reduce(jnp.pad(part, wide), jnp.pad(labels, wide))[:, :outs]
    k_nystrom = kernel_of(points, points_sq, batch, batch_sq)
    pulled = jnp.dot(k_nystrom, resid, preferred_element_type=jnp.float32)
    projected = lax.dot_general(
        eig, pulled, (((0,), (0,)), ((), ())), precision=lax.Precision.HIGHEST
    )
    gradient = jnp.dot(k_batch, resid, preferred_element_type=jnp.float32)
    corrected = jnp.dot(
        eig, corrections[:, None] * projected, precision=lax.Precision.HIGHEST
    ).astype(jnp.bfloat16)
    tile = kernel_of(centers, center_sq, points, points_sq)
    nystrom_term = jnp.dot(tile, corrected, preferred_element_type=jnp.float32)
    return weights - RATE / 512 * (gradient - nystrom_term)


def solution(mesh):
    every = P(("narrow", "wide", "nys"), None)
    some = P(("narrow", "nys"), None)
    return jax.shard_map(
        per_device,
        mesh=mesh,
        in_specs=(every, every, every, every, some, some, P()),
        out_specs=every,
        check_vma=False,
    )
```

time: 1290 us -> 177 us (0.14); the launches traced: 1270 us -> 177 us
  waiting for transfers between devices: 1120 us -> 0 us
  Pallas kernels: 0 us -> 103 us
  blocking collectives: 82.7 us -> 0 us
  matrix products: 33.3 us -> 63.8 us
  between operations: 13.2 us -> 0.12 us
    all_gather x3 -> x0, waiting for transfers between devices: 841 us -> none  [the longest x1 525 us: per_device(): lax.all_gather(batch_points, ('narrow', 'wide', 'nys'), axis=0, tiled=True)]
    psum x1 -> x0, waiting for transfers between devices: 280 us -> none  [per_device(): projected = lax.psum(local_proj, ('narrow', 'nys'))]
    pallas_call x0 -> x2, Pallas kernels: none -> 103 us  [the longest x1 53.5 us: gather(): pl.pallas_call(gather_kernel, out_shape=(jax.ShapeDtypeStruct((512, 1024)...]
    psum x1 -> x0, blocking collectives: 82.7 us -> none  [per_device(): lax.psum(partial_value - placed, ('narrow', 'wide', 'nys'))]
    dot_general x6, matrix products: 30.7 us -> 62.5 us  [the longest x1 16.3 us: per_device(): nystrom_term = jnp.dot(tile, corrected, preferred_element_type=jnp.float32)]
  transfers between devices with their start and end apart: 4 -> 0, of which waited for: 4 -> 0; matrix products, arithmetic and copies ran while one was open for 1% -> 0% of each run, Pallas kernels for 0% -> 0%
where the time goes in v1:
time: 177 us
  Pallas kernels  103 us (58%)
  matrix products  63.8 us (36%)
  local copies, waits for them, and re-layouts  6.6 us (4%)
  other arithmetic  3.88 us (2%)
    pallas_call x1, Pallas kernels, gather(): pl.pallas_call(gather_kernel, out_shape=(jax.ShapeDtypeStruct((512, 1024)...  53.5 us
    pallas_call x1, Pallas kernels, reduce(): pl.pallas_call(reduce_kernel, out_shape=jax.ShapeDtypeStruct((512, 1024),...  49.3 us
    dot_general x1, matrix products, per_device(): nystrom_term = jnp.dot(tile, corrected, preferred_element_type=jnp.float32)  16.3 us
    dot_general x1, matrix products, per_device(): lax.dot_general(eig, pulled, (((0,), (0,)), ((), ())), precision=lax.Prec...  16 us
    dot_general x1, matrix products, per_device(): pulled = jnp.dot(k_nystrom, resid, preferred_element_type=jnp.float32)  11.2 us
    dot_general x1, matrix products, per_device(): jnp.dot(eig, corrections[:, None] * projected, precision=lax.Precision.HI...  8.41 us
    dot_general x1, matrix products, per_device(): gradient = jnp.dot(k_batch, resid, preferred_element_type=jnp.float32)  6.72 us
    reduce_sum x3, other arithmetic, squares(): return jnp.sum(jnp.square(points.astype(jnp.float32)), axis=1)  3.88 us

profile of v1, /device:TPU:1, one launch (start us, length us, event | category | flops | bytes accessed | tf_op | source)
XLA Modules:
  0.0 177.2 jit_solution(8205777812321857453)
XLA Ops:
  0.0 2.1 %multiply_reduce_fusion.1 = f32[1024]{0:T(1024)S(1)} fusion(bf16[1024,1024]{1,0:T(8,128)(2,1)} %param.7), kind=kLoop, calls=%fused_computation.9 | loop fusion | flops 3144704 | bytes 2101248 | tf_op jit(solution)/shard_map/reduce_sum | solution.py:285
  2.1 0.7 reshape.16.batch
  2.8 0.7 pad.14.labels
  3.5 0.8 pad.12.eig
  4.3 0.0 copy-start.1
  4.3 0.9 copy-done.1
  5.2 53.5 %gather.1 = (bf16[512,1024]{1,0:T(8,128)(2,1)S(1)}, bf16[2048,1024]{1,0:T(8,128)(2,1)S(1)}, f32[2048,256]{1,0:T(8,128)S(1)}) custom-call(bf16[16,128]{1,0:T(8,128)(2,1)S(1)} %reshape.16.batch, bf16[64,1024]{1,0:T(8,128)(2,1)S(1)} %copy-done.1, f32[64,256]{1,0:T(8,128)S(1)} %pad.12.eig), custom_call_target="tpu_custom_call" | custom-call | tf_op jit(solution)/shard_map/gather/pallas_call | solution.py:163
  58.8 0.0 copy-start
  58.8 2.0 %copy-done = bf16[2048,1024]{1,0:T(8,128)(2,1)} copy-done((bf16[2048,1024]{1,0:T(8,128)(2,1)}, bf16[2048,1024]{1,0:T(8,128)(2,1)S(1)}, u32[]{:S(2)}) %copy-start) | copy-done | bytes 4194328
  60.8 0.9 multiply_reduce_fusion
  61.7 0.9 multiply_reduce_fusion.2
  62.6 0.1 add.48
  62.7 0.2 copy.11
  62.9 0.0 copy-start.5
  62.9 1.0 copy-done.5
  63.9 0.0 copy-start.2
  63.9 3.9 %fusion.13 = bf16[1024,512]{0,1:T(8,128)(2,1)S(1)} fusion(bf16[1024,1024]{1,0:T(8,128)(2,1)} %param.7, f32[512]{0:T(512)S(1)} %add.48, f32[1024]{0:T(1024)S(1)} %multiply_reduce_fusion.1, bf16[64,8,8,128]{3,2,1,0:T(8,128)(2,1)S(1)} %bitcast.64), kind=kOutput, calls=%fused_computation.19 | convolution fusion | flops 1077411840 | bytes 4200448 | tf_op jit(solution)/shard_map/dot_general | solution.py:276
  67.8 0.0 copy-done.2
  67.8 0.0 copy-start.3
  67.8 1.3 fusion.20
  69.1 0.0 copy-done.3
  69.1 0.1 pad.13.part
  69.3 49.3 %reduce.2 = bf16[512,1024]{1,0:T(8,128)(2,1)S(1)} custom-call(f32[512,1024]{1,0:T(8,128)S(1)} %pad.13.part, f32[2,1024]{1,0:T(2,128)S(1)} %pad.14.labels), custom_call_target="tpu_custom_call" | custom-call | tf_op jit(solution)/shard_map/reduce/pallas_call | solution.py:252
  118.6 0.0 copy-start.6
  118.6 11.2 %fusion.29 = f32[2048,1000]{0,1:T(8,128)} fusion(bf16[2048,1024]{1,0:T(8,128)(2,1)} %copy-done, f32[512]{0:T(512)S(1)} %add.48, f32[2048]{0:T(1024)S(1)} %multiply_reduce_fusion, bf16[64,8,8,128]{3,2,1,0:T(8,128)(2,1)} %bitcast.65, bf16[512,1024]{1,0:T(8,128)(2,1)S(1)} %reduce.2), kind=kOutput, calls=%fused_computation.31 | convolution fusion | flops 4251975680 | bytes 14493696 | tf_op jit(solution)/shard_map/dot_general | solution.py:312
  129.8 0.0 copy-done.6
  129.8 16.0 %fusion.23 = f32[160,1000]{1,0:T(8,128)S(1)} fusion(f32[2048,1000]{0,1:T(8,128)} %fusion.29, f32[2048,256]{1,0:T(8,128)S(1)} %get-tuple-element.10, f32[160]{0:T(256)S(1)} %copy-done.6), kind=kOutput, calls=%fused_computation.28 | convolution fusion | flops 3932320000 | bytes 10929792 | tf_op jit(solution)/shard_map/dot_general | solution.py:313
  145.9 8.4 %fusion.16 = bf16[2048,1000]{0,1:T(8,128)(2,1)} fusion(f32[160,1000]{1,0:T(8,128)S(1)} %fusion.23, f32[2048,256]{1,0:T(8,128)S(1)} %get-tuple-element.10), kind=kOutput, calls=%fused_computation.23 | convolution fusion | flops 3932160000 | bytes 6833152 | tf_op jit(solution)/shard_map/dot_general | solution.py:317
  154.3 0.0 copy-start.4
  154.3 16.3 %fusion.40 = f32[1024,1000]{0,1:T(8,128)} fusion(bf16[2048,1000]{0,1:T(8,128)(2,1)} %fusion.16, bf16[2048,1024]{1,0:T(8,128)(2,1)} %copy-done, bf16[1024,1024]{1,0:T(8,128)(2,1)} %param.7, f32[2048]{0:T(1024)S(1)} %multiply_reduce_fusion, f32[1024]{0:T(1024)S(1)} %multiply_reduce_fusion.1), kind=kOutput, calls=%fused_computation.40 | convolution fusion | flops 8503951360 | bytes 14495744 | tf_op jit(solution)/shard_map/dot_general | solution.py:321
  170.5 0.0 copy-done.4
  170.5 6.7 %multiply_subtract_fusion = f32[1024,1000]{0,1:T(8,128)} fusion(f32[1024,1000]{0,1:T(8,128)} %param.8, f32[1024,1000]{0,1:T(8,128)} %fusion.40, bf16[1024,512]{0,1:T(8,128)(2,1)S(1)} %copy-done.4, bf16[512,1024]{1,0:T(8,128)(2,1)S(1)} %reduce.2), kind=kOutput, calls=%fused_computation.10 | convolution fusion | flops 1051648000 | bytes 14385152 | tf_op jit(solution)/shard_map/dot_general | solution.py:316
Async XLA Ops:
  4.3 0.9 copy-start.1
  58.8 2.0 %copy-start = (bf16[2048,1024]{1,0:T(8,128)(2,1)}, bf16[2048,1024]{1,0:T(8,128)(2,1)S(1)}, u32[]{:S(2)}) copy-start(bf16[2048,1024]{1,0:T(8,128)(2,1)S(1)} %get-tuple-element.9) | copy-start | bytes 12582916
  62.9 1.0 copy-start.5
  63.9 3.9 %copy-start.2 = (f32[1024,1000]{0,1:T(8,128)S(1)}, f32[1024,1000]{0,1:T(8,128)}, u32[]{:S(2)}) copy-start(f32[1024,1000]{0,1:T(8,128)} %param.8) | copy-start | bytes 12288004
  67.8 1.3 copy-start.3
  118.6 11.2 %copy-start.6 = (f32[160]{0:T(256)S(1)}, f32[160]{0:T(256)}, u32[]{:S(2)}) copy-start(f32[160]{0:T(256)} %param.13) | copy-start | bytes 1924
  154.3 16.3 %copy-start.4 = (bf16[1024,512]{0,1:T(8,128)(2,1)S(1)}, bf16[1024,512]{0,1:T(8,128)(2,1)}, u32[]{:S(2)}) copy-start(bf16[1024,512]{0,1:T(8,128)(2,1)} %copy-done.3) | copy-start | bytes 3145732

commit v2 on v0

v2 whole, which is shorter than its diff:
```python
import math

import jax
import jax.numpy as jnp
from jax import lax
from jax.experimental import pallas as pl
from jax.experimental.pallas import tpu as pltpu
from jax.sharding import PartitionSpec as P

RATE = 16.0
SPREAD = 4.0
MESH = pl.DeviceIdType.MESH
F32, BF16 = jnp.float32, jnp.bfloat16

FEATURES = 1024
CEN = 1024
OUT = 1000
NYS = 2048
BATCH = 512
Q = 160
UNIT = (math.log2(math.e) / SPREAD) ** 2
TOP = math.sqrt(2.0 * FEATURES) * math.log2(math.e) / SPREAD


def device(x, y, z, c):
    return (y * 2 + z % 2, (z // 2) * 2 + c, x)


class Links:
    def __init__(self, send, recv):
        n, w, self.x = (lax.axis_index(a) for a in ("narrow", "wide", "nys"))
        self.y, self.c = n // 2, w % 2
        self.z = (w // 2) * 2 + n % 2
        self.p = self.x * (1 - self.c) + self.y * self.c
        self.q = self.y * (1 - self.c) + self.x * self.c
        self.send, self.recv, self.next, self.all = send, recv, 0, []

    def core(self):
        return device(self.x, self.y, self.z, 1 - self.c)

    def along_p(self, k):
        c = self.c
        return device((self.x + k * (1 - c)) % 4, (self.y + k * c) % 4, self.z, c)

    def along_q(self, k):
        c = self.c
        return device((self.x + k * c) % 4, (self.y + k * (1 - c)) % 4, self.z, c)

    def along_z(self, k):
        return device(self.x, self.y, (self.z + k) % 8, self.c)

    def z_pair(self):
        return device(self.x, self.y, self.z + 1 - 2 * (self.z % 2), self.c)

    def peers(self):
        out = [self.core()]
        out += [self.along_p(k) for k in range(1, 4)]
        out += [self.along_q(k) for k in range(1, 4)]
        out += [self.along_z(k) for k in range(1, 8)]
        return out

    def start(self, pairs):
        out = []
        for src, dst, peer in pairs:
            copy = pltpu.make_async_remote_copy(
                src_ref=src,
                dst_ref=dst,
                send_sem=self.send.at[self.next],
                recv_sem=self.recv.at[self.next],
                device_id=peer,
                device_id_type=MESH,
            )
            self.next += 1
            copy.start()
            out.append(copy)
        self.all += out
        return out


def arrived(copies):
    for copy in copies:
        copy.wait_recv()


def at(start, size, unit=None):
    if isinstance(start, int):
        return slice(start, start + size)
    return pl.ds(pl.multiple_of(start, unit or size), size)


def square_sums(points):
    wide = points.astype(F32)
    return jnp.sum(wide * wide, axis=1, keepdims=True) * UNIT


def as_row(column):
    return jnp.transpose(jnp.broadcast_to(column, (column.shape[0], 128)))[0:1, :]


def kernel_values(left, left_sq, right, right_sq):
    cross = lax.dot_general(left, right, (((1,), (1,)), ((), ())), preferred_element_type=F32)
    dist_sq = jnp.maximum((left_sq + right_sq) - (2.0 * UNIT) * cross, 1e-30)
    return jnp.exp2(TOP - dist_sq * lax.rsqrt(dist_sq)).astype(BF16)


def three(value):
    high = value.astype(BF16)
    rest = value - high.astype(F32)
    middle = rest.astype(BF16)
    low = (rest - middle.astype(F32)).astype(BF16)
    return high, middle, low


def step_kernel(
    centers,
    weights,
    batch,
    labels,
    nystrom,
    eigvecs,
    corrections,
    out,
    left,
    left_sq,
    right,
    right_sq,
    center_sq,
    small_batch,
    small_labels,
    small_eig,
    small_corr,
    tiles,
    wide_tiles,
    wide_batch,
    old,
    rounded,
    eig,
    stack,
    k_batch,
    part,
    sum1,
    sum2,
    from_p,
    from_q,
    from_z,
    table,
    mixed,
    mixed_t,
    coefs,
    tail_in,
    send,
    recv,
    local,
):
    links = Links(send, recv)
    c, p, q, z = links.c, links.p, links.q, links.z
    group = p * 4 + q

    own_n = c * 1024 + p * 256 + q * 64 + (z % 2) * 32
    loads = [
        (batch, small_batch),
        (labels, small_labels),
        (eigvecs, small_eig),
        (nystrom.at[at(c * 32, 32), :], right.at[at(own_n, 32), :]),
        (centers, left.at[0:1024, :]),
        (weights, old),
        (corrections, small_corr),
    ]
    loads = [pltpu.make_async_copy(s, d, local.at[i]) for i, (s, d) in enumerate(loads)]
    for load in loads:
        load.start()
    barrier = pltpu.get_barrier_semaphore()
    peers = links.peers()
    for peer in peers:
        pl.semaphore_signal(barrier, inc=1, device_id=peer, device_id_type=MESH)

    loads[0].wait()
    pair = small_batch[...].astype(F32)
    for r in range(2):
        for j in range(8):
            wide_tiles[0, 8 * r + j : 8 * r + j + 1, :] = pair[r : r + 1, 128 * j : 128 * j + 128]
    tiles[at(group * 16, 16), at(z * 128, 128)] = wide_tiles[0, 0:16, :].astype(BF16)
    loads[1].wait()
    loads[2].wait()
    eig[at(own_n, 32), :] = jnp.zeros((32, 256), F32)
    eig[at(own_n, 32), 0:Q] = small_eig[at(c * 32, 32), :]
    loads[3].wait()
    pl.semaphore_wait(barrier, len(peers))

    def gather_z(ref, first):
        tile = ref.at[at(first + group * 16, 16), at(z * 128, 128)]
        return links.start([(tile, tile, links.along_z(k)) for k in range(1, 8)])

    def gather_q(ref, first):
        block = ref.at[at(first + group * 16, 16), :]
        return links.start([(block, block, links.along_q(k)) for k in range(1, 4)])

    def gather_p(ref, first):
        block = ref.at[at(first + p * 64, 64), :]
        return links.start([(block, block, links.along_p(k)) for k in range(1, 4)])

    batch_z = gather_z(tiles, 0)
    own = [r.at[at(own_n, 32), :] for r in (right, eig)]
    nys_z = links.start([(o, o, links.z_pair()) for o in own])
    loads[4].wait()
    swap = links.start([(left.at[0:1024, :], left.at[1280:2304, :], links.core())])

    arrived(batch_z)
    batch_q = gather_q(tiles, 0)
    arrived(nys_z)
    own = [r.at[at(c * 1024 + p * 256 + q * 64, 64), :] for r in (right, eig)]
    nys_q = links.start([(o, o, links.along_q(k)) for k in range(1, 4) for o in own])

    loads[5].wait()
    rounded[0:1024, 896:1024] = jnp.zeros((1024, 128), BF16)

    def round_rows(i, carry):
        rows = at(i * 128, 128)
        rounded[rows, 0:OUT] = old[rows, :].astype(BF16)
        return carry

    lax.fori_loop(0, 8, round_rows, 0)
    swap += links.start([(rounded.at[0:1024, :], rounded.at[1024:2048, :], links.core())])

    arrived(batch_q)
    batch_p = gather_p(tiles, 0)

    def own_squares(i, carry):
        rows = at(i * 256, 256)
        value = square_sums(left[rows, :])
        left_sq[rows, :] = value
        center_sq[:, rows] = as_row(value)
        return carry

    lax.fori_loop(0, 4, own_squares, 0)
    arrived(nys_q)
    blocks = [c * 1024 + ((p + k) % 4) * 256 for k in range(4)]
    block = right.at[at(blocks[0], 256), :]
    nys_own = links.start([(block, block, links.core())])
    arrived(swap)

    def other_squares(i, carry):
        rows = pl.ds(pl.multiple_of(1280 + i * 256, 256), 256)
        center_sq[:, at(1024 + i * 256, 256)] = as_row(square_sums(left[rows, :]))
        return carry

    lax.fori_loop(0, 4, other_squares, 0)
    arrived(batch_p)
    own = [r.at[at(blocks[0], 256), :] for r in (right, eig)]
    nys_p = links.start([(o, o, links.along_p(k)) for k in (1, 3) for o in own[:1]])
    eig_p = links.start([(own[1], own[1], links.along_p(k)) for k in (1, 2, 3)])

    for zz in range(8):
        wide_tiles[zz] = tiles[:, 128 * zz : 128 * zz + 128].astype(F32)
    for zz in range(8):
        for j in range(8):
            wide_batch[j, pl.ds(zz, 32, stride=8), :] = wide_tiles[zz, pl.ds(j, 32, stride=8), :]
    squares = jnp.zeros((256, 128), F32)
    for j in range(8):
        wide = wide_batch[j]
        left[1024:1280, 128 * j : 128 * j + 128] = wide.astype(BF16)
        squares = squares + wide * wide
    left_sq[1024:1280, :] = jnp.sum(squares, axis=1, keepdims=True) * UNIT
    right[at(2048 + c * 256, 256), :] = left[1024:1280, :]
    block = right.at[at(2048 + c * 256, 256), :]
    batch_own = links.start([(block, block, links.core())])
    points, points_sq = left[1024:1280, :], left_sq[1024:1280, :]
    for i in range(8):
        first = i * 256 if i < 4 else 256 + i * 256
        k_batch[:, 256 * i : 256 * i + 256] = kernel_values(
            points, points_sq, left[first : first + 256, :], center_sq[:, 256 * i : 256 * i + 256]
        )
    scale = (CEN * 256) ** (-0.5)
    for i in range(4):
        cols = slice(256 * i, 256 * i + 256)
        part[:, cols] = scale * jnp.dot(k_batch[...], rounded[:, cols], preferred_element_type=F32)
    sum_p = links.start(
        [
            (part.at[at(((p + k) % 4) * 64, 64), :], from_p.at[k - 1], links.along_p(k))
            for k in range(1, 4)
        ]
    )

    def fill(first, height):
        cols = at(first, 256)
        if not isinstance(first, int):
            cols = pl.ds(pl.multiple_of(first, 256), 256)
        right_sq[:, cols] = as_row(square_sums(right[cols, :]))

        def body(i, carry):
            rows = at(i * (height // 2), height // 2)
            table[rows, cols] = kernel_values(
                left[rows, :], left_sq[rows, :], right[cols, :], right_sq[:, cols]
            )
            return carry

        lax.fori_loop(0, 2, body, 0)

    theirs = [(1 - c) * 1024 + ((q + k) % 4) * 256 for k in range(4)]
    fill(blocks[0], 1280)
    arrived(nys_own)
    fill(theirs[0], 1280)
    arrived(nys_p)
    nys_core = links.start(
        [
            (right.at[at(blocks[k], 256), :], right.at[at(blocks[k], 256), :], links.core())
            for k in (1, 3)
        ]
    )
    fill(blocks[1], 1280)
    fill(blocks[3], 1280)
    arrived(batch_own)

    arrived(sum_p)
    nys_far = links.start([(own[0], own[0], links.along_p(2))])
    arrived(eig_p)
    half = eig.at[at(c * 1024, 1024), :]
    eig_core = links.start([(half, half, links.core())])

    def add_p(i, carry):
        rows = at(i * 16, 16)
        sum1[rows, :] = (
            part[at(p * 64 + i * 16, 16), :]
            + from_p[0, rows, :]
            + from_p[1, rows, :]
            + from_p[2, rows, :]
        )
        return carry

    lax.fori_loop(0, 4, add_p, 0)
    line = lax.broadcasted_iota(jnp.int32, (16, OUT), 0)
    placed = jnp.where(
        line == z, small_labels[0:1, :], jnp.where(line == z + 8, small_labels[1:2, :], 0.0)
    )
    sum1[at(q * 16, 16), 0:OUT] = sum1[at(q * 16, 16), 0:OUT] - placed
    sum_q = links.start(
        [
            (sum1.at[at(((q + k) % 4) * 16, 16), :], from_q.at[k - 1], links.along_q(k))
            for k in range(1, 4)
        ]
    )
    arrived(nys_core)
    fill(theirs[1], 1280)
    fill(theirs[3], 1280)
    arrived(sum_q)
    sum2[...] = sum1[at(q * 16, 16), :] + from_q[0] + from_q[1] + from_q[2]
    sum_z = links.start(
        [
            (sum2.at[:, at(((z + k) % 8) * 128, 128)], from_z.at[k - 1], links.along_z(k))
            for k in range(1, 8)
        ]
    )
    arrived(nys_far)
    block = right.at[at(blocks[2], 256), :]
    nys_last = links.start([(block, block, links.core())])
    fill(2048, 1024)
    fill(2304, 1024)
    fill(blocks[2], 1280)
    arrived(sum_z)
    total = sum2[:, at(z * 128, 128)]
    for k in range(7):
        total = total + from_z[k]
    coefs[at(2048 + c * 256 + group * 16, 16), at(z * 128, 128)] = total.astype(BF16)
    first = 2048 + c * 256
    resid_z = gather_z(coefs, first)

    arrived(nys_last)
    fill(theirs[2], 1280)
    arrived(eig_core)

    def split(i, carry):
        rows = at(i * 256, 256)
        a = three(eig[rows, 0:128])
        high, middle, low = (v.astype(F32) for v in three(eig[rows, 128:256]))
        for j, v in enumerate((0, 0, 1, 0, 1, 2)):
            stack[rows, 128 * j : 128 * j + 128] = a[v]
        stack[rows, 768:896] = (
            high
            + pltpu.roll(high, 32, 1)
            + pltpu.roll(middle, 64, 1)
            + pltpu.roll(high, 96, 1)
        ).astype(BF16)
        stack[rows, 896:1024] = (middle + pltpu.roll(low, 32, 1)).astype(BF16)
        return carry

    lax.fori_loop(0, 8, split, 0)
    arrived(resid_z)
    resid_q = gather_q(coefs, first)

    loads[6].wait()
    mixed_rows = at(c * 256, 256)
    product = jnp.dot(table[1024:1280, 0:NYS], stack[...], preferred_element_type=F32)
    mixed[mixed_rows, 0:128] = (
        product[:, 0:128] + product[:, 256:384] + product[:, 640:768]
    ) * small_corr[:, 0:128]
    last = product[:, 768:896]
    last = last + pltpu.roll(last, 64, 1) + pltpu.roll(product[:, 896:1024], 96, 1)
    mixed[mixed_rows, 128:Q] = last[:, 0 : Q - 128] * small_corr[:, 128:Q]
    half = mixed.at[mixed_rows, :]
    mixed_core = links.start([(half, half, links.core())])
    arrived(resid_q)
    resid_p = gather_p(coefs, first)
    block = coefs.at[at(first + p * 64, 64), :]
    resid_core = links.start([(block, block, links.core())])
    arrived(mixed_core)
    turned = jnp.transpose(mixed[...])[0:Q, :]
    for i, piece in enumerate(three(turned)):
        mixed_t[Q * i : Q * i + Q, :] = piece
    for k, copy in zip((1, 2, 3), resid_p):
        arrived([copy])
        block = coefs.at[at(first + ((p + 4 - k) % 4) * 64, 64), :]
        resid_core += links.start([(block, block, links.core())])
    arrived(resid_core)

    for i in range(4):
        cols = slice(256 * i, 256 * i + 256)
        resid = coefs[2048:2560, cols]
        pieces = jnp.dot(mixed_t[...], resid, preferred_element_type=F32)
        pieces = three(pieces[0:Q] + pieces[Q : 2 * Q] + pieces[2 * Q : 3 * Q])
        for j, v in enumerate((0, 1, 0, 2, 1, 0)):
            tail_in[128 * j : 128 * j + 128, :] = pieces[v][0:128]
            tail_in[768 + 32 * j : 800 + 32 * j, :] = pieces[v][128:Q]
        tail_in[960:1024, :] = jnp.zeros((64, 256), BF16)

        def correct(k, carry):
            rows = at(k * 512, 512)
            coefs[rows, cols] = -jnp.dot(
                stack[rows, :], tail_in[...], preferred_element_type=F32
            ).astype(BF16)
            return carry

        lax.fori_loop(0, 4, correct, 0)
        kept = slice(256 * i, min(256 * i + 256, OUT))

        def finish(k, carry):
            rows = at(k * 512, 512)
            change = jnp.dot(table[rows, :], coefs[:, cols], preferred_element_type=F32)
            out[rows, kept] = old[rows, kept] - (RATE / BATCH) * change[:, 0 : kept.stop - kept.start]
            return carry

        lax.fori_loop(0, 2, finish, 0)
    for copy in links.all:
        copy.wait_send()


def per_device(centers, weights, batch_points, labels, nystrom_points, eigvecs, corrections):
    anywhere = pl.BlockSpec(memory_space=pl.ANY)
    vmem = pltpu.VMEM
    return pl.pallas_call(
        step_kernel,
        out_shape=jax.ShapeDtypeStruct((CEN, OUT), F32),
        in_specs=[anywhere] * 7,
        out_specs=pl.BlockSpec(memory_space=vmem),
        scratch_shapes=[
            vmem((2304, FEATURES), BF16),
            vmem((1280, 1), F32),
            vmem((2560, FEATURES), BF16),
            vmem((1, 2560), F32),
            vmem((1, 2048), F32),
            vmem((2, FEATURES), BF16),
            vmem((2, OUT), F32),
            vmem((64, Q), F32),
            vmem((1, Q), F32),
            vmem((256, FEATURES), BF16),
            vmem((8, 256, 128), F32),
            vmem((8, 256, 128), F32),
            vmem((CEN, OUT), F32),
            vmem((2048, 1024), BF16),
            vmem((NYS, 256), F32),
            vmem((NYS, 1024), BF16),
            vmem((256, 2048), BF16),
            vmem((256, 1024), F32),
            vmem((64, 1024), F32),
            vmem((16, 1024), F32),
            vmem((3, 64, 1024), F32),
            vmem((3, 16, 1024), F32),
            vmem((7, 16, 128), F32),
            vmem((1280, 2560), BF16),
            vmem((BATCH, 256), F32),
            vmem((3 * Q, BATCH), BF16),
            vmem((2560, 1024), BF16),
            vmem((1024, 256), BF16),
            pltpu.SemaphoreType.DMA((80,)),
            pltpu.SemaphoreType.DMA((80,)),
            pltpu.SemaphoreType.DMA((7,)),
        ],
        compiler_params=pltpu.CompilerParams(
            collective_id=0, has_side_effects=True, vmem_limit_bytes=60 << 20
        ),
        name="step",
    )(
        centers,
        weights,
        batch_points,
        labels,
        nystrom_points,
        eigvecs,
        corrections.reshape(1, Q),
    )


def solution(mesh):
    every = P(("narrow", "wide", "nys"), None)
    some = P(("narrow", "nys"), None)
    return jax.shard_map(
        per_device,
        mesh=mesh,
        in_specs=(every, every, every, every, some, some, P()),
        out_specs=every,
        check_vma=False,
    )
```

time: 1290 us -> 107 us (0.08); the launches traced: 1270 us -> 107 us
  waiting for transfers between devices: 1120 us -> 0 us
  Pallas kernels: 0 us -> 96.5 us
  blocking collectives: 82.7 us -> 0 us
  matrix products: 33.3 us -> 0 us
  between operations: 13.2 us -> 0.01 us
    all_gather x3 -> x0, waiting for transfers between devices: 841 us -> none  [the longest x1 525 us: per_device(): lax.all_gather(batch_points, ('narrow', 'wide', 'nys'), axis=0, tiled=True)]
    psum x1 -> x0, waiting for transfers between devices: 280 us -> none  [per_device(): projected = lax.psum(local_proj, ('narrow', 'nys'))]
    pallas_call x0 -> x1, Pallas kernels: none -> 96.5 us  [per_device(): pl.pallas_call(step_kernel, out_shape=jax.ShapeDtypeStruct((CEN, OUT), F3...]
    psum x1 -> x0, blocking collectives: 82.7 us -> none  [per_device(): lax.psum(partial_value - placed, ('narrow', 'wide', 'nys'))]
    dot_general x7 -> x0, matrix products: 33.3 us -> none  [the longest x1 15.5 us: per_device(): nystrom_term = jnp.dot(tile, coefs, preferred_element_type=jnp.float32)]
  transfers between devices with their start and end apart: 4 -> 0, of which waited for: 4 -> 0; matrix products, arithmetic and copies ran while one was open for 1% -> 0% of each run, Pallas kernels for 0% -> 0%
where the time goes in v2:
time: 107 us
  Pallas kernels  96.5 us (90%)
  local copies, waits for them, and re-layouts  10.7 us (10%)
    pallas_call x1, Pallas kernels, per_device(): pl.pallas_call(step_kernel, out_shape=jax.ShapeDtypeStruct((CEN, OUT), F3...  96.5 us
    unnamed x1, local copies, waits for them, and re-layouts  5.33 us
    pallas_call x1, local copies, waits for them, and re-layouts, per_device(): pl.pallas_call(step_kernel, out_shape=jax.ShapeDtypeStruct((CEN, OUT), F3...  5.32 us

profile of v2, /device:TPU:1, one launch (start us, length us, event | category | flops | bytes accessed | tf_op | source)
XLA Modules:
  0.0 107.2 jit_solution(5564302658843959765)
XLA Ops:
  0.0 5.3 %copy.8.weights = f32[1024,1000]{1,0:T(8,128)} copy(f32[1024,1000]{0,1:T(8,128)} %param.8) | data formatting | bytes 8192000 | tf_op args[1]
  5.3 96.5 %step.1 = f32[1024,1000]{1,0:T(8,128)} custom-call(bf16[1024,1024]{1,0:T(8,128)(2,1)} %centers.1, f32[1024,1000]{1,0:T(8,128)} %copy.8.weights, bf16[2,1024]{1,0:T(2,128)(2,1)} %batch.1, f32[2,1000]{1,0:T(2,128)} %labels.1, bf16[64,1024]{1,0:T(8,128)(2,1)} %nystrom.1, f32[64,160]{1,0:T(8,128)} %eigvecs.1, f32[1,160]{1,0:T(1,128)} %bitcast.1), custom_call_target="tpu_custom_call" | custom-call | tf_op jit(solution)/shard_map/step/pallas_call | solution.py:449
  101.8 5.3 %copy.9 = f32[1024,1000]{0,1:T(8,128)} copy(f32[1024,1000]{1,0:T(8,128)} %step.1) | data formatting | bytes 8192000 | tf_op jit(solution)/shard_map/step/pallas_call | solution.py:449

commit v3 on v2

v3 whole, which is shorter than its diff:
```python
import math

import jax
import jax.numpy as jnp
from jax import lax
from jax.experimental import pallas as pl
from jax.experimental.pallas import tpu as pltpu
from jax.sharding import PartitionSpec as P

RATE = 16.0
SPREAD = 4.0
MESH = pl.DeviceIdType.MESH
F32, BF16 = jnp.float32, jnp.bfloat16

FEATURES = 1024
CEN = 1024
OUT = 1000
NYS = 2048
BATCH = 512
Q = 160
UNIT = (math.log2(math.e) / SPREAD) ** 2
TOP = math.sqrt(2.0 * FEATURES) * math.log2(math.e) / SPREAD


def device(x, y, z, c):
    return (y * 2 + z % 2, (z // 2) * 2 + c, x)


class Links:
    def __init__(self, send, recv):
        n, w, self.x = (lax.axis_index(a) for a in ("narrow", "wide", "nys"))
        self.y, self.c = n // 2, w % 2
        self.z = (w // 2) * 2 + n % 2
        self.p = self.x * (1 - self.c) + self.y * self.c
        self.q = self.y * (1 - self.c) + self.x * self.c
        self.send, self.recv, self.next, self.all = send, recv, 0, []

    def core(self):
        return device(self.x, self.y, self.z, 1 - self.c)

    def along_p(self, k):
        c = self.c
        return device((self.x + k * (1 - c)) % 4, (self.y + k * c) % 4, self.z, c)

    def along_q(self, k):
        c = self.c
        return device((self.x + k * c) % 4, (self.y + k * (1 - c)) % 4, self.z, c)

    def along_z(self, k):
        return device(self.x, self.y, (self.z + k) % 8, self.c)

    def z_pair(self):
        return device(self.x, self.y, self.z + 1 - 2 * (self.z % 2), self.c)

    def peers(self):
        out = [self.core()]
        out += [self.along_p(k) for k in range(1, 4)]
        out += [self.along_q(k) for k in range(1, 4)]
        out += [self.along_z(k) for k in range(1, 8)]
        return out

    def start(self, pairs):
        out = []
        for src, dst, peer in pairs:
            copy = pltpu.make_async_remote_copy(
                src_ref=src,
                dst_ref=dst,
                send_sem=self.send.at[self.next],
                recv_sem=self.recv.at[self.next],
                device_id=peer,
                device_id_type=MESH,
            )
            self.next += 1
            copy.start()
            out.append(copy)
        self.all += out
        return out


def arrived(copies):
    for copy in copies:
        copy.wait_recv()


def at(start, size, unit=None):
    if isinstance(start, int):
        return slice(start, start + size)
    return pl.ds(pl.multiple_of(start, unit or size), size)


def square_sums(points):
    wide = points.astype(F32)
    return jnp.sum(wide * wide, axis=1, keepdims=True) * UNIT


def as_row(column):
    return jnp.transpose(jnp.broadcast_to(column, (column.shape[0], 128)))[0:1, :]


def kernel_values(left, left_sq, right, right_sq):
    cross = lax.dot_general(left, right, (((1,), (1,)), ((), ())), preferred_element_type=F32)
    dist_sq = jnp.maximum((left_sq + right_sq) - (2.0 * UNIT) * cross, 1e-30)
    return jnp.exp2(TOP - dist_sq * lax.rsqrt(dist_sq)).astype(BF16)


def three(value):
    high = value.astype(BF16)
    rest = value - high.astype(F32)
    middle = rest.astype(BF16)
    low = (rest - middle.astype(F32)).astype(BF16)
    return high, middle, low


def step_kernel(
    centers,
    weights,
    batch,
    labels,
    nystrom,
    eigvecs,
    corrections,
    out,
    left,
    left_sq,
    right,
    right_sq,
    center_sq,
    small_batch,
    small_labels,
    small_eig,
    small_corr,
    tiles,
    wide_tiles,
    wide_batch,
    old,
    rounded,
    eig,
    stack,
    k_batch,
    part,
    placed,
    sum1,
    sum2,
    from_p,
    from_q,
    from_z,
    table,
    mixed,
    coefs,
    scaled,
    send,
    recv,
    local,
):
    links = Links(send, recv)
    c, p, q, z = links.c, links.p, links.q, links.z
    group = p * 4 + q

    own_n = c * 1024 + p * 256 + q * 64 + (z % 2) * 32
    loads = [
        (batch, small_batch),
        (labels, small_labels),
        (eigvecs, small_eig),
        (nystrom.at[at(c * 32, 32), :], right.at[at(own_n, 32), :]),
        (centers, left.at[0:1024, :]),
        (weights, old),
        (corrections, small_corr),
    ]
    loads = [pltpu.make_async_copy(s, d, local.at[i]) for i, (s, d) in enumerate(loads)]
    for load in loads:
        load.start()
    barrier = pltpu.get_barrier_semaphore()
    peers = links.peers()
    for peer in peers:
        pl.semaphore_signal(barrier, inc=1, device_id=peer, device_id_type=MESH)

    loads[0].wait()
    pair = small_batch[...].astype(F32)
    for r in range(2):
        for j in range(8):
            wide_tiles[0, 8 * r + j : 8 * r + j + 1, :] = pair[r : r + 1, 128 * j : 128 * j + 128]
    tiles[at(group * 16, 16), at(z * 128, 128)] = wide_tiles[0, 0:16, :].astype(BF16)
    loads[2].wait()
    own_e = own_n // 32
    mine = small_eig[at(c * 32, 32), :]
    eig[own_e, 0:32, :] = mine[:, 0:128]
    for k in range(4):
        eig[own_e, 32:40, 32 * k : 32 * k + 32] = mine[8 * k : 8 * k + 8, 128:Q]
    loads[3].wait()
    pl.semaphore_wait(barrier, len(peers))

    def nys(first, count):
        return right.at[at(first, count, count), :]

    def vectors(first, count):
        return eig.at[pl.ds(first // 32, count // 32)]

    tile = tiles.at[at(group * 16, 16), at(z * 128, 128)]
    batch_q = links.start([(tile, tile, links.along_q(k)) for k in range(1, 4)])
    own = [nys(own_n, 32), vectors(own_n, 32)]
    nys_z = links.start([(o, o, links.z_pair()) for o in own])
    loads[4].wait()
    swap = links.start([(left.at[0:1024, :], left.at[1280:2304, :], links.core())])

    arrived(batch_q)
    tile = tiles.at[at(p * 64, 64), at(z * 128, 128)]
    batch_z = links.start([(tile, tile, links.along_z(k)) for k in range(1, 8)])
    arrived(nys_z)
    own_q = c * 1024 + p * 256 + q * 64
    own = [nys(own_q, 64), vectors(own_q, 64)]
    nys_q = links.start([(o, o, links.along_q(k)) for k in range(1, 4) for o in own])

    loads[5].wait()
    for i in range(7):
        rows = slice(128 * i, 128 * i + 128)
        rounded[rows, 0:1024] = old[rows, :].astype(BF16)
    last = jnp.concatenate([old[896:OUT, :], jnp.zeros((1024 - OUT, CEN), F32)], axis=0)
    rounded[896:1024, 0:1024] = last.astype(BF16)
    swap += links.start([(rounded.at[:, 0:1024], rounded.at[:, 1024:2048], links.core())])

    arrived(batch_z)
    block = tiles.at[at(p * 64, 64), :]
    batch_p = links.start([(block, block, links.along_p(k)) for k in range(1, 4)])

    def own_squares(i, carry):
        rows = at(i * 256, 256)
        value = square_sums(left[rows, :])
        left_sq[rows, :] = value
        center_sq[:, rows] = as_row(value)
        return carry

    lax.fori_loop(0, 4, own_squares, 0)
    loads[1].wait()
    wide_labels = [
        jnp.transpose(jnp.broadcast_to(small_labels[r : r + 1, :], (128, OUT))) for r in range(2)
    ]
    lane = lax.broadcasted_iota(jnp.int32, (OUT, 128), 1)
    for i in range(2):
        point = group * 16 + z - 128 * i
        placed[0:OUT, 128 * i : 128 * i + 128] = jnp.where(
            lane == point, wide_labels[0], jnp.where(lane == point + 8, wide_labels[1], 0.0)
        )
    placed[OUT:1024, :] = jnp.zeros((1024 - OUT, 256), F32)
    arrived(nys_q)
    blocks = [c * 1024 + ((p + k) % 4) * 256 for k in range(4)]
    nys_own = links.start([(nys(blocks[0], 256), nys(blocks[0], 256), links.core())])
    arrived(swap)

    def other_squares(i, carry):
        rows = pl.ds(pl.multiple_of(1280 + i * 256, 256), 256)
        center_sq[:, pl.ds(pl.multiple_of(1024 + i * 256, 256), 256)] = as_row(
            square_sums(left[rows, :])
        )
        return carry

    lax.fori_loop(0, 4, other_squares, 0)
    arrived(batch_p)
    piece = [nys(blocks[0] + 128 * i, 128) for i in range(2)]
    nys_p = links.start([(piece[0], piece[0], links.along_p(k)) for k in (1, 3)])

    for zz in range(8):
        wide_tiles[zz] = tiles[:, 128 * zz : 128 * zz + 128].astype(F32)
    for zz in range(8):
        for j in range(8):
            wide_batch[j, pl.ds(zz, 32, stride=8), :] = wide_tiles[zz, pl.ds(j, 32, stride=8), :]
    squares = jnp.zeros((256, 128), F32)
    for j in range(8):
        wide = wide_batch[j]
        left[1024:1280, 128 * j : 128 * j + 128] = wide.astype(BF16)
        squares = squares + wide * wide
    left_sq[1024:1280, :] = jnp.sum(squares, axis=1, keepdims=True) * UNIT
    points, points_sq = left[1024:1280, :], left_sq[1024:1280, :]
    for i in range(8):
        first = i * 256 if i < 4 else 256 + i * 256
        k_batch[:, 256 * i : 256 * i + 256] = kernel_values(
            points, points_sq, left[first : first + 256, :], center_sq[:, 256 * i : 256 * i + 256]
        )
    scale = (CEN * 256) ** (-0.5)
    for i in range(4):
        rows = slice(256 * i, 256 * i + 256)
        part[rows, :] = scale * by_rows(rounded[rows, :], k_batch[...]) - placed[rows, :]
    sum_p = links.start(
        [
            (part.at[at(((p + k) % 4) * 256, 256), :], from_p.at[k - 1], links.along_p(k))
            for k in range(1, 4)
        ]
    )
    own_b = at(2048 + c * 256, 256)
    right[own_b, :] = left[1024:1280, :]
    batch_own = links.start([(right.at[own_b, :], right.at[own_b, :], links.core())])

    def fill(first, height):
        cols = pl.ds(pl.multiple_of(first, 256), 256)
        right_sq[:, cols] = as_row(square_sums(right[cols, :]))
        for i in range(2):
            rows = slice(i * (height // 2), (i + 1) * (height // 2))
            table[rows, cols] = kernel_values(
                left[rows, :], left_sq[rows, :], right[cols, :], right_sq[:, cols]
            )

    theirs = [(1 - c) * 1024 + ((q + k) % 4) * 256 for k in range(4)]
    fill(blocks[0], 1280)
    arrived(nys_own)
    fill(theirs[0], 1280)
    fill(2048 + c * 256, 1024)
    arrived(batch_own)
    fill(2304 - c * 256, 1024)

    arrived(sum_p)
    for i in range(4):
        rows = slice(64 * i, 64 * i + 64)
        sum1[rows, :] = (
            part[at(p * 256 + 64 * i, 64), :]
            + from_p[0, rows, :]
            + from_p[1, rows, :]
            + from_p[2, rows, :]
        )
    sum_q = links.start(
        [
            (sum1.at[at(((q + k) % 4) * 64, 64), :], from_q.at[k - 1], links.along_q(k))
            for k in range(1, 4)
        ]
    )
    nys_p += links.start([(piece[1], piece[1], links.along_p(k)) for k in (1, 3)])
    mine = vectors(blocks[0], 256)
    eig_p = links.start([(mine, mine, links.along_p(k)) for k in range(1, 4)])

    arrived(sum_q)
    sum2[...] = sum1[at(q * 64, 64), :] + from_q[0] + from_q[1] + from_q[2]

    def share(ref, first, owner, col=0):
        return ref.at[at(first + (owner // 2) * 16, 16), at(col + (owner % 2) * 128, 128)]

    sum_z = links.start(
        [
            (share(sum2, 0, (z + k) % 8), from_z.at[k - 1], links.along_z(k))
            for k in range(1, 8)
        ]
    )
    nys_far = links.start([(nys(blocks[0], 256), nys(blocks[0], 256), links.along_p(2))])
    arrived(nys_p)
    nys_core = links.start(
        [(nys(blocks[k], 256), nys(blocks[k], 256), links.core()) for k in (1, 3)]
    )
    fill(blocks[1], 1280)
    fill(blocks[3], 1280)

    arrived(sum_z)
    total = share(sum2, 0, z)[...]
    for k in range(7):
        total = total + from_z[k]
    here = at(2048 + c * 256, 256)
    tile = share(coefs, p * 256 + q * 64, z, 2048 + c * 256)
    tile[...] = total.astype(BF16)
    resid_z = links.start([(tile, tile, links.along_z(k)) for k in range(1, 8)])
    arrived(nys_core)
    fill(theirs[1], 1280)
    fill(theirs[3], 1280)
    arrived(eig_p)
    eig_core = links.start([(vectors(c * 1024, 1024), vectors(c * 1024, 1024), links.core())])

    arrived(resid_z)
    tile = coefs.at[at(p * 256 + q * 64, 64), here]
    resid_q = links.start([(tile, tile, links.along_q(k)) for k in range(1, 4)])
    arrived(nys_far)
    nys_last = links.start([(nys(blocks[2], 256), nys(blocks[2], 256), links.core())])
    fill(blocks[2], 1280)
    arrived(eig_core)

    narrow = lax.broadcasted_iota(jnp.int32, (256, 128), 1) < 32

    def split(i, carry):
        rows = at(i * 256, 256)
        some = eig[pl.ds(i * 8, 8), :, :]
        high, middle, low = three(some[:, 0:32, :].reshape(256, 128))
        stack[rows, 0:128] = high
        stack[rows, 128:256] = high
        stack[rows, 256:384] = middle
        stack[rows, 512:640] = low
        rest = some[:, 32:40, :].reshape(64, 128)
        rest = [rest] + [pltpu.roll(rest, 128 - 32 * k, 1) for k in range(1, 4)]
        rest = jnp.concatenate([v.reshape(8, 8, 128) for v in rest], axis=1).reshape(256, 128)
        high, middle, low = three(jnp.where(narrow, rest, 0.0))
        stack[rows, 384:512] = beside(high, high, middle)
        stack[rows, 640:768] = low
        return carry

    lax.fori_loop(0, 8, split, 0)
    arrived(resid_q)
    tile = coefs.at[at(p * 256, 256), here]
    resid_p = links.start([(tile, tile, links.along_p(k)) for k in range(1, 4)])
    resid_core = links.start([(tile, tile, links.core())])
    arrived(nys_last)
    fill(theirs[2], 1280)

    loads[6].wait()
    product = jnp.dot(table[1024:1280, 0:NYS], stack[...], preferred_element_type=F32)
    value = product[:, 0:128] + product[:, 256:384] + product[:, 512:640]
    high, middle, low = three(value * small_corr[:, 0:128])
    rows = at(c * 256, 256)
    mixed[rows, 0:128] = high
    mixed[rows, 128:256] = middle
    mixed[rows, 256:384] = low
    value = product[:, 384:512]
    value = value + pltpu.roll(value, 64, 1) + product[:, 640:768]
    high, middle, low = three(jnp.where(narrow, value * small_corr[:, 128:256], 0.0))
    mixed[rows, 384:512] = beside(high, middle, low)
    mixed_core = links.start([(mixed.at[rows, :], mixed.at[rows, :], links.core())])
    for k, copy in zip((1, 2, 3), resid_p):
        arrived([copy])
        tile = coefs.at[at(((p + 4 - k) % 4) * 256, 256), here]
        resid_core += links.start([(tile, tile, links.core())])
    arrived(mixed_core)
    arrived(resid_core)

    narrow = lax.broadcasted_iota(jnp.int32, (1024, 128), 1) < 32
    value = jnp.dot(coefs[:, 2048:2560], mixed[...], preferred_element_type=F32)
    high, middle, _ = three(value[:, 0:128] + value[:, 128:256] + value[:, 256:384])
    scaled[:, 0:128] = high
    scaled[:, 128:256] = middle
    scaled[:, 256:384] = high
    value = value[:, 384:512]
    value = value + pltpu.roll(value, 96, 1) + pltpu.roll(value, 64, 1)
    high, middle, _ = three(jnp.where(narrow, value, 0.0))
    scaled[:, 384:512] = beside(high, middle, high)
    for i in range(4):
        cols = slice(512 * i, 512 * i + 512)
        for k in range(2):
            rows = slice(512 * k, 512 * k + 512)
            coefs[rows, cols] = (-by_rows(scaled[rows, :], stack[cols, 0:512])).astype(BF16)
    for i in range(4):
        cols = slice(256 * i, 256 * i + 256)
        for rows in (slice(0, 512), slice(512, OUT)):
            change = by_rows(coefs[rows.start : rows.start + 512, :], table[cols, :])
            out[rows, cols] = old[rows, cols] - (RATE / BATCH) * change[0 : rows.stop - rows.start]
    for copy in links.all:
        copy.wait_send()


def by_rows(a, b):
    return lax.dot_general(a, b, (((1,), (1,)), ((), ())), preferred_element_type=F32)


def beside(a, b, c):
    a, b, c = (v.astype(F32) for v in (a, b, c))
    return (a + pltpu.roll(b, 32, 1) + pltpu.roll(c, 64, 1)).astype(BF16)


def per_device(centers, weights, batch_points, labels, nystrom_points, eigvecs, corrections):
    anywhere = pl.BlockSpec(memory_space=pl.ANY)
    vmem = pltpu.VMEM
    return pl.pallas_call(
        step_kernel,
        out_shape=jax.ShapeDtypeStruct((OUT, CEN), F32),
        in_specs=[anywhere] * 7,
        out_specs=pl.BlockSpec(memory_space=vmem),
        scratch_shapes=[
            vmem((2304, FEATURES), BF16),
            vmem((1280, 1), F32),
            vmem((2560, FEATURES), BF16),
            vmem((1, 2560), F32),
            vmem((1, 2048), F32),
            vmem((2, FEATURES), BF16),
            vmem((2, OUT), F32),
            vmem((64, Q), F32),
            vmem((1, 256), F32),
            vmem((256, FEATURES), BF16),
            vmem((8, 256, 128), F32),
            vmem((8, 256, 128), F32),
            vmem((OUT, CEN), F32),
            vmem((1024, 2048), BF16),
            vmem((64, 40, 128), F32),
            vmem((NYS, 768), BF16),
            vmem((256, 2048), BF16),
            vmem((1024, 256), F32),
            vmem((1024, 256), F32),
            vmem((256, 256), F32),
            vmem((64, 256), F32),
            vmem((3, 256, 256), F32),
            vmem((3, 64, 256), F32),
            vmem((7, 16, 128), F32),
            vmem((1280, 2560), BF16),
            vmem((BATCH, 512), BF16),
            vmem((1024, 2560), BF16),
            vmem((1024, 512), BF16),
            pltpu.SemaphoreType.DMA((80,)),
            pltpu.SemaphoreType.DMA((80,)),
            pltpu.SemaphoreType.DMA((7,)),
        ],
        compiler_params=pltpu.CompilerParams(
            collective_id=0, has_side_effects=True, vmem_limit_bytes=60 << 20
        ),
        name="step",
    )(
        centers,
        weights.T,
        batch_points,
        labels,
        nystrom_points,
        eigvecs,
        jnp.pad(corrections, (0, 256 - Q)).reshape(1, 256),
    ).T


def solution(mesh):
    every = P(("narrow", "wide", "nys"), None)
    some = P(("narrow", "nys"), None)
    return jax.shard_map(
        per_device,
        mesh=mesh,
        in_specs=(every, every, every, every, some, some, P()),
        out_specs=every,
        check_vma=False,
    )
```

time: 107 us -> 83.1 us (0.78)
  Pallas kernels: 96.5 us -> 77.1 us
  local copies, waits for them, and re-layouts: 10.7 us -> 5.94 us
    pallas_call x1, Pallas kernels: 96.5 us -> 77.1 us  [per_device(): pl.pallas_call(step_kernel, out_shape=jax.ShapeDtypeStruct((OUT, CEN), F3...]
    pallas_call x1 -> x0, local copies, waits for them, and re-layouts: 5.32 us -> none  [per_device(): pl.pallas_call(step_kernel, out_shape=jax.ShapeDtypeStruct((CEN, OUT), F3...]
    pad x0 -> x1, local copies, waits for them, and re-layouts: none -> 1.24 us  [per_device(): jnp.pad(corrections, (0, 256 - Q)).reshape(1, 256)]
where the time goes in v3:
time: 83.1 us; the launch traced here: 83 us
  Pallas kernels  77.1 us (93%)
  local copies, waits for them, and re-layouts  5.94 us (7%)
    pallas_call x1, Pallas kernels, per_device(): pl.pallas_call(step_kernel, out_shape=jax.ShapeDtypeStruct((OUT, CEN), F3...  77.1 us
    unnamed x1, local copies, waits for them, and re-layouts  4.7 us

profile of v3, /device:TPU:1, one launch (start us, length us, event | category | flops | bytes accessed | tf_op | source)
XLA Modules:
  0.0 83.0 jit_solution(6240316154264682522)
XLA Ops:
  0.0 1.2 %pad.4 = f32[256]{0:T(256)} pad(f32[160]{0:T(256)} %param.13, f32[]{:T(128)} %constant.2.clone.1), padding=0_96 | pad | bytes 1668 | tf_op jit(solution)/shard_map/jit(_pad)/pad | solution.py:501
  1.2 77.1 %step.1 = f32[1000,1024]{1,0:T(8,128)} custom-call(bf16[1024,1024]{1,0:T(8,128)(2,1)} %centers.1, f32[1000,1024]{1,0:T(8,128)} %bitcast.4, bf16[2,1024]{1,0:T(2,128)(2,1)} %batch.1, f32[2,1000]{1,0:T(2,128)} %labels.1, bf16[64,1024]{1,0:T(8,128)(2,1)} %nystrom.1, f32[64,160]{1,0:T(8,128)} %eigvecs.1, f32[1,256]{1,0:T(1,128)} %bitcast.5), custom_call_target="tpu_custom_call" | custom-call | tf_op jit(solution)/shard_map/step/pallas_call | solution.py:452
  78.3 4.7 %copy.9 = f32[1024,1000]{0,1:T(8,128)} copy(f32[1024,1000]{0,1:T(8,128)} %bitcast.3) | data formatting | bytes 8192000

commit v4 on v3

--- a/solution.py
+++ b/solution.py
@@ -129,6 +129,7 @@
     small_labels,
     small_eig,
     small_corr,
+    wide_corr,
     tiles,
     wide_tiles,
     wide_batch,
@@ -144,6 +145,7 @@
     from_p,
     from_q,
     from_z,
+    gathered,
     table,
     mixed,
     coefs,
@@ -276,15 +278,23 @@
             points, points_sq, left[first : first + 256, :], center_sq[:, 256 * i : 256 * i + 256]
         )
     scale = (CEN * 256) ** (-0.5)
-    for i in range(4):
-        rows = slice(256 * i, 256 * i + 256)
-        part[rows, :] = scale * by_rows(rounded[rows, :], k_batch[...]) - placed[rows, :]
-    sum_p = links.start(
-        [
-            (part.at[at(((p + k) % 4) * 256, 256), :], from_p.at[k - 1], links.along_p(k))
-            for k in range(1, 4)
-        ]
-    )
+    sum_p = []
+    for h in range(2):
+        for i in range(2):
+            rows = slice(512 * h + 256 * i, 512 * h + 256 * i + 256)
+            part[rows, :] = scale * by_rows(rounded[rows, :], k_batch[...]) - placed[rows, :]
+        sum_p.append(
+            links.start(
+                [
+                    (
+                        part.at[at(512 * h + ((p + k) % 4) * 128, 128), :],
+                        from_p.at[h, k - 1],
+                        links.along_p(k),
+                    )
+                    for k in range(1, 4)
+                ]
+            )
+        )
     own_b = at(2048 + c * 256, 256)
     right[own_b, :] = left[1024:1280, :]
     batch_own = links.start([(right.at[own_b, :], right.at[own_b, :], links.core())])
@@ -299,72 +309,111 @@
             )
 
     theirs = [(1 - c) * 1024 + ((q + k) % 4) * 256 for k in range(4)]
+    here = at(2048 + c * 256, 256)
+
+    def start_sum_q(h):
+        arrived(sum_p[h])
+        for i in range(2):
+            rows = slice(64 * i, 64 * i + 64)
+            sum1[h, rows, :] = (
+                part[at(512 * h + p * 128 + 64 * i, 64), :]
+                + from_p[h, 0, rows, :]
+                + from_p[h, 1, rows, :]
+                + from_p[h, 2, rows, :]
+            )
+        return links.start(
+            [
+                (
+                    sum1.at[h, at(((q + k) % 4) * 32, 32), :],
+                    from_q.at[h, k - 1],
+                    links.along_q(k),
+                )
+                for k in range(1, 4)
+            ]
+        )
+
+    def share(h, owner):
+        return sum2.at[h, at((owner // 2) * 8, 8), at((owner % 2) * 128, 128)]
+
+    def start_sum_z(h):
+        arrived(sum_q[h])
+        sum2[h] = sum1[h, at(q * 32, 32), :] + from_q[h, 0] + from_q[h, 1] + from_q[h, 2]
+        return links.start(
+            [
+                (share(h, (z + k) % 8), from_z.at[h, k - 1], links.along_z(k))
+                for k in range(1, 8)
+            ]
+        )
+
+    def start_resid_z(h):
+        arrived(sum_z[h])
+        total = share(h, z)[...]
+        for k in range(7):
+            total = total + from_z[h, k]
+        gathered[h, z] = total
+        tile = gathered.at[h, z]
+        return links.start([(tile, tile, links.along_z(k)) for k in range(1, 8)])
+
+    def resid_rows(h, first, count):
+        return coefs.at[at(512 * h + first, count), here]
+
+    def start_resid_q(h):
+        arrived(resid_z[h])
+        rows = [
+            jnp.concatenate([gathered[h, 2 * i], gathered[h, 2 * i + 1]], axis=1) for i in range(4)
+        ]
+        tile = resid_rows(h, p * 128 + q * 32, 32)
+        tile[...] = jnp.concatenate(rows, axis=0).astype(BF16)
+        return links.start([(tile, tile, links.along_q(k)) for k in range(1, 4)])
+
+    def start_resid_p(h):
+        arrived(resid_q[h])
+        tile = resid_rows(h, p * 128, 128)
+        out = links.start([(tile, tile, links.along_p(k)) for k in range(1, 4)])
+        return out, links.start([(tile, tile, links.core())])
+
+    def pass_on(h):
+        copies, more = resid_p[h]
+        for k, copy in zip((1, 2, 3), copies):
+            arrived([copy])
+            tile = resid_rows(h, ((p + 4 - k) % 4) * 128, 128)
+            more += links.start([(tile, tile, links.core())])
+        return more
+
     fill(blocks[0], 1280)
     arrived(nys_own)
     fill(theirs[0], 1280)
+    sum_q = [start_sum_q(0)]
     fill(2048 + c * 256, 1024)
-    arrived(batch_own)
-    fill(2304 - c * 256, 1024)
-
-    arrived(sum_p)
-    for i in range(4):
-        rows = slice(64 * i, 64 * i + 64)
-        sum1[rows, :] = (
-            part[at(p * 256 + 64 * i, 64), :]
-            + from_p[0, rows, :]
-            + from_p[1, rows, :]
-            + from_p[2, rows, :]
-        )
-    sum_q = links.start(
-        [
-            (sum1.at[at(((q + k) % 4) * 64, 64), :], from_q.at[k - 1], links.along_q(k))
-            for k in range(1, 4)
-        ]
-    )
+    sum_q.append(start_sum_q(1))
     nys_p += links.start([(piece[1], piece[1], links.along_p(k)) for k in (1, 3)])
     mine = vectors(blocks[0], 256)
     eig_p = links.start([(mine, mine, links.along_p(k)) for k in range(1, 4)])
-
-    arrived(sum_q)
-    sum2[...] = sum1[at(q * 64, 64), :] + from_q[0] + from_q[1] + from_q[2]
-
-    def share(ref, first, owner, col=0):
-        return ref.at[at(first + (owner // 2) * 16, 16), at(col + (owner % 2) * 128, 128)]
-
-    sum_z = links.start(
-        [
-            (share(sum2, 0, (z + k) % 8), from_z.at[k - 1], links.along_z(k))
-            for k in range(1, 8)
-        ]
-    )
+    arrived(batch_own)
+    fill(2304 - c * 256, 1024)
+    sum_z = [start_sum_z(0)]
+    sum_z.append(start_sum_z(1))
     nys_far = links.start([(nys(blocks[0], 256), nys(blocks[0], 256), links.along_p(2))])
+    resid_z = [start_resid_z(0)]
+    resid_z.append(start_resid_z(1))
     arrived(nys_p)
     nys_core = links.start(
         [(nys(blocks[k], 256), nys(blocks[k], 256), links.core()) for k in (1, 3)]
     )
     fill(blocks[1], 1280)
     fill(blocks[3], 1280)
-
-    arrived(sum_z)
-    total = share(sum2, 0, z)[...]
-    for k in range(7):
-        total = total + from_z[k]
-    here = at(2048 + c * 256, 256)
-    tile = share(coefs, p * 256 + q * 64, z, 2048 + c * 256)
-    tile[...] = total.astype(BF16)
-    resid_z = links.start([(tile, tile, links.along_z(k)) for k in range(1, 8)])
     arrived(nys_core)
     fill(theirs[1], 1280)
     fill(theirs[3], 1280)
+    resid_q = [start_resid_q(0)]
+    resid_q.append(start_resid_q(1))
     arrived(eig_p)
     eig_core = links.start([(vectors(c * 1024, 1024), vectors(c * 1024, 1024), links.core())])
-
-    arrived(resid_z)
-    tile = coefs.at[at(p * 256 + q * 64, 64), here]
-    resid_q = links.start([(tile, tile, links.along_q(k)) for k in range(1, 4)])
     arrived(nys_far)
     nys_last = links.start([(nys(blocks[2], 256), nys(blocks[2], 256), links.core())])
     fill(blocks[2], 1280)
+    resid_p = [start_resid_p(0)]
+    resid_p.append(start_resid_p(1))
     arrived(eig_core)
 
     narrow = lax.broadcasted_iota(jnp.int32, (256, 128), 1) < 32
@@ -386,53 +435,58 @@
         return carry
 
     lax.fori_loop(0, 8, split, 0)
-    arrived(resid_q)
-    tile = coefs.at[at(p * 256, 256), here]
-    resid_p = links.start([(tile, tile, links.along_p(k)) for k in range(1, 4)])
-    resid_core = links.start([(tile, tile, links.core())])
     arrived(nys_last)
     fill(theirs[2], 1280)
 
     loads[6].wait()
+    wide_corr[...] = jnp.zeros((1, 256), F32)
+    wide_corr[:, 0:Q] = small_corr[...]
     product = jnp.dot(table[1024:1280, 0:NYS], stack[...], preferred_element_type=F32)
     value = product[:, 0:128] + product[:, 256:384] + product[:, 512:640]
-    high, middle, low = three(value * small_corr[:, 0:128])
+    high, middle, low = three(value * wide_corr[:, 0:128])
     rows = at(c * 256, 256)
     mixed[rows, 0:128] = high
     mixed[rows, 128:256] = middle
     mixed[rows, 256:384] = low
     value = product[:, 384:512]
     value = value + pltpu.roll(value, 64, 1) + product[:, 640:768]
-    high, middle, low = three(jnp.where(narrow, value * small_corr[:, 128:256], 0.0))
+    high, middle, low = three(jnp.where(narrow, value * wide_corr[:, 128:256], 0.0))
     mixed[rows, 384:512] = beside(high, middle, low)
     mixed_core = links.start([(mixed.at[rows, :], mixed.at[rows, :], links.core())])
-    for k, copy in zip((1, 2, 3), resid_p):
-        arrived([copy])
-        tile = coefs.at[at(((p + 4 - k) % 4) * 256, 256), here]
-        resid_core += links.start([(tile, tile, links.core())])
+    narrow = lax.broadcasted_iota(jnp.int32, (512, 128), 1) < 32
+
+    def project(h):
+        rows = slice(512 * h, 512 * h + 512)
+        value = jnp.dot(coefs[rows, 2048:2560], mixed[...], preferred_element_type=F32)
+        high, middle, _ = three(value[:, 0:128] + value[:, 128:256] + value[:, 256:384])
+        scaled[rows, 0:128] = high
+        scaled[rows, 128:256] = middle
+        scaled[rows, 256:384] = high
+        value = value[:, 384:512]
+        value = value + pltpu.roll(value, 96, 1) + pltpu.roll(value, 64, 1)
+        high, middle, _ = three(jnp.where(narrow, value, 0.0))
+        scaled[rows, 384:512] = beside(high, middle, high)
+
+    def finish(h):
+        rows = slice(512 * h, 512 * h + 512)
+        for i in range(4):
+            cols = slice(512 * i, 512 * i + 512)
+            coefs[rows, cols] = (-by_rows(scaled[rows, :], stack[cols, 0:512])).astype(BF16)
+        kept = min(512, OUT - 512 * h)
+        for i in range(4):
+            cols = slice(256 * i, 256 * i + 256)
+            change = by_rows(coefs[rows, :], table[cols, :])
+            out[512 * h : 512 * h + kept, cols] = (RATE / BATCH) * change[0:kept]
+
+    resid_core = pass_on(0)
     arrived(mixed_core)
     arrived(resid_core)
-
-    narrow = lax.broadcasted_iota(jnp.int32, (1024, 128), 1) < 32
-    value = jnp.dot(coefs[:, 2048:2560], mixed[...], preferred_element_type=F32)
-    high, middle, _ = three(value[:, 0:128] + value[:, 128:256] + value[:, 256:384])
-    scaled[:, 0:128] = high
-    scaled[:, 128:256] = middle
-    scaled[:, 256:384] = high
-    value = value[:, 384:512]
-    value = value + pltpu.roll(value, 96, 1) + pltpu.roll(value, 64, 1)
-    high, middle, _ = three(jnp.where(narrow, value, 0.0))
-    scaled[:, 384:512] = beside(high, middle, high)
-    for i in range(4):
-        cols = slice(512 * i, 512 * i + 512)
-        for k in range(2):
-            rows = slice(512 * k, 512 * k + 512)
-            coefs[rows, cols] = (-by_rows(scaled[rows, :], stack[cols, 0:512])).astype(BF16)
-    for i in range(4):
-        cols = slice(256 * i, 256 * i + 256)
-        for rows in (slice(0, 512), slice(512, OUT)):
-            change = by_rows(coefs[rows.start : rows.start + 512, :], table[cols, :])
-            out[rows, cols] = old[rows, cols] - (RATE / BATCH) * change[0 : rows.stop - rows.start]
+    project(0)
+    resid_core = pass_on(1)
+    finish(0)
+    arrived(resid_core)
+    project(1)
+    finish(1)
     for copy in links.all:
         copy.wait_send()
 
@@ -447,12 +501,12 @@
 
 
 def per_device(centers, weights, batch_points, labels, nystrom_points, eigvecs, corrections):
-    anywhere = pl.BlockSpec(memory_space=pl.ANY)
+    hbm = pl.BlockSpec(memory_space=pltpu.HBM)
     vmem = pltpu.VMEM
-    return pl.pallas_call(
+    change = pl.pallas_call(
         step_kernel,
         out_shape=jax.ShapeDtypeStruct((OUT, CEN), F32),
-        in_specs=[anywhere] * 7,
+        in_specs=[hbm] * 7,
         out_specs=pl.BlockSpec(memory_space=vmem),
         scratch_shapes=[
             vmem((2304, FEATURES), BF16),
@@ -463,6 +517,7 @@
             vmem((2, FEATURES), BF16),
             vmem((2, OUT), F32),
             vmem((64, Q), F32),
+            vmem((1, Q), F32),
             vmem((1, 256), F32),
             vmem((256, FEATURES), BF16),
             vmem((8, 256, 128), F32),
@@ -474,32 +529,39 @@
             vmem((256, 2048), BF16),
             vmem((1024, 256), F32),
             vmem((1024, 256), F32),
-            vmem((256, 256), F32),
-            vmem((64, 256), F32),
-            vmem((3, 256, 256), F32),
-            vmem((3, 64, 256), F32),
-            vmem((7, 16, 128), F32),
+            vmem((2, 128, 256), F32),
+            vmem((2, 32, 256), F32),
+            vmem((2, 3, 128, 256), F32),
+            vmem((2, 3, 32, 256), F32),
+            vmem((2, 7, 8, 128), F32),
+            vmem((2, 8, 8, 128), F32),
             vmem((1280, 2560), BF16),
             vmem((BATCH, 512), BF16),
             vmem((1024, 2560), BF16),
             vmem((1024, 512), BF16),
-            pltpu.SemaphoreType.DMA((80,)),
-            pltpu.SemaphoreType.DMA((80,)),
+            pltpu.SemaphoreType.DMA((110,)),
+            pltpu.SemaphoreType.DMA((110,)),
             pltpu.SemaphoreType.DMA((7,)),
         ],
         compiler_params=pltpu.CompilerParams(
-            collective_id=0, has_side_effects=True, vmem_limit_bytes=60 << 20
+            collective_id=0, has_side_effects=True, vmem_limit_bytes=50 << 20
         ),
         name="step",
     )(
-        centers,
-        weights.T,
-        batch_points,
-        labels,
-        nystrom_points,
-        eigvecs,
-        jnp.pad(corrections, (0, 256 - Q)).reshape(1, 256),
-    ).T
+        *(
+            pltpu.with_memory_space_constraint(v, pltpu.HBM)
+            for v in (
+                centers,
+                weights.T,
+                batch_points,
+                labels,
+                nystrom_points,
+                eigvecs,
+                corrections.reshape(1, Q),
+            )
+        )
+    )
+    return (weights.T - change).T
 
 
 def solution(mesh):

time: 83.1 us -> 78.1 us (0.940)
  local copies, waits for them, and re-layouts: 5.94 us -> 0.01 us
  other arithmetic: 0 us -> 3.31 us
  Pallas kernels: 77.1 us -> 74.7 us
    unnamed x1 -> x2, local copies, waits for them, and re-layouts: 4.7 us -> 0.01 us
    transpose x0 -> x1, other arithmetic: none -> 3.31 us  [per_device(): return (weights.T - change).T]
    pallas_call x1, Pallas kernels: 77.1 us -> 74.7 us  [per_device(): pl.pallas_call(step_kernel, out_shape=jax.ShapeDtypeStruct((OUT, CEN), F3...]
    pad x1 -> x0, local copies, waits for them, and re-layouts: 1.24 us -> none  [per_device(): jnp.pad(corrections, (0, 256 - Q)).reshape(1, 256)]
where the time goes in v4:
time: 78.1 us; the launch traced here: 78 us
  Pallas kernels  74.7 us (96%)
  other arithmetic  3.31 us (4%)
    pallas_call x1, Pallas kernels, per_device(): pl.pallas_call(step_kernel, out_shape=jax.ShapeDtypeStruct((OUT, CEN), F3...  74.7 us
    transpose x1, other arithmetic, per_device(): return (weights.T - change).T  3.31 us

profile of v4, /device:TPU:1, one launch (start us, length us, event | category | flops | bytes accessed | tf_op | source)
XLA Modules:
  0.0 78.0 jit_solution(13829704189241705194)
XLA Ops:
  0.0 0.0 copy-start
  0.0 74.7 %step.1 = f32[1000,1024]{1,0:T(8,128)S(1)} custom-call(bf16[1024,1024]{1,0:T(8,128)(2,1)} %centers.1, f32[1000,1024]{1,0:T(8,128)} %bitcast.5, bf16[2,1024]{1,0:T(2,128)(2,1)} %batch.1, f32[2,1000]{1,0:T(2,128)} %labels.1, bf16[64,1024]{1,0:T(8,128)(2,1)} %nystrom.1, f32[64,160]{1,0:T(8,128)} %eigvecs.1, f32[1,160]{1,0:T(1,128)} %bitcast.6), custom_call_target="tpu_custom_call" | custom-call | tf_op jit(solution)/shard_map/step/pallas_call | solution.py:506
  74.7 0.0 copy-done
  74.7 3.3 %subtract_bitcast_fusion = f32[1024,1000]{0,1:T(8,128)} fusion(f32[1000,1024]{1,0:T(8,128)S(1)} %step.1, f32[1024,1000]{0,1:T(8,128)S(1)} %copy-done), kind=kLoop, calls=%fused_computation | loop fusion | flops 1024000 | bytes 12288000 | tf_op jit(solution)/shard_map/transpose | solution.py:564
Async XLA Ops:
  0.0 74.7 %copy-start = (f32[1024,1000]{0,1:T(8,128)S(1)}, f32[1024,1000]{0,1:T(8,128)}, u32[]{:S(2)}) copy-start(f32[1024,1000]{0,1:T(8,128)} %param.8) | copy-start | bytes 12288004

commit v5 on v4

--- a/solution.py
+++ b/solution.py
@@ -119,7 +119,10 @@
     nystrom,
     eigvecs,
     corrections,
-    out,
+    stack,
+    table,
+    mixed,
+    resid,
     left,
     left_sq,
     right,
@@ -136,7 +139,6 @@
     old,
     rounded,
     eig,
-    stack,
     k_batch,
     part,
     placed,
@@ -146,10 +148,6 @@
     from_q,
     from_z,
     gathered,
-    table,
-    mixed,
-    coefs,
-    scaled,
     send,
     recv,
     local,
@@ -158,7 +156,7 @@
     c, p, q, z = links.c, links.p, links.q, links.z
     group = p * 4 + q
 
-    own_n = c * 1024 + p * 256 + q * 64 + (z % 2) * 32
+    own_n = c * 1024 + p * 256 + (z % 2) * 128 + q * 32
     loads = [
         (batch, small_batch),
         (labels, small_labels),
@@ -198,19 +196,19 @@
         return eig.at[pl.ds(first // 32, count // 32)]
 
     tile = tiles.at[at(group * 16, 16), at(z * 128, 128)]
-    batch_q = links.start([(tile, tile, links.along_q(k)) for k in range(1, 4)])
+    batch_z = links.start([(tile, tile, links.along_z(k)) for k in range(1, 8)])
     own = [nys(own_n, 32), vectors(own_n, 32)]
-    nys_z = links.start([(o, o, links.z_pair()) for o in own])
+    nys_q = links.start([(o, o, links.along_q(k)) for k in range(1, 4) for o in own])
     loads[4].wait()
     swap = links.start([(left.at[0:1024, :], left.at[1280:2304, :], links.core())])
 
-    arrived(batch_q)
-    tile = tiles.at[at(p * 64, 64), at(z * 128, 128)]
-    batch_z = links.start([(tile, tile, links.along_z(k)) for k in range(1, 8)])
-    arrived(nys_z)
-    own_q = c * 1024 + p * 256 + q * 64
-    own = [nys(own_q, 64), vectors(own_q, 64)]
-    nys_q = links.start([(o, o, links.along_q(k)) for k in range(1, 4) for o in own])
+    arrived(batch_z)
+    tile = tiles.at[at(group * 16, 16), :]
+    batch_q = links.start([(tile, tile, links.along_q(k)) for k in range(1, 4)])
+    arrived(nys_q)
+    own_z = c * 1024 + p * 256 + (z % 2) * 128
+    own = [nys(own_z, 128), vectors(own_z, 128)]
+    nys_z = links.start([(o, o, links.z_pair()) for o in own])
 
     loads[5].wait()
     for i in range(7):
@@ -220,7 +218,7 @@
     rounded[896:1024, 0:1024] = last.astype(BF16)
     swap += links.start([(rounded.at[:, 0:1024], rounded.at[:, 1024:2048], links.core())])
 
-    arrived(batch_z)
+    arrived(batch_q)
     block = tiles.at[at(p * 64, 64), :]
     batch_p = links.start([(block, block, links.along_p(k)) for k in range(1, 4)])
 
@@ -243,9 +241,7 @@
             lane == point, wide_labels[0], jnp.where(lane == point + 8, wide_labels[1], 0.0)
         )
     placed[OUT:1024, :] = jnp.zeros((1024 - OUT, 256), F32)
-    arrived(nys_q)
     blocks = [c * 1024 + ((p + k) % 4) * 256 for k in range(4)]
-    nys_own = links.start([(nys(blocks[0], 256), nys(blocks[0], 256), links.core())])
     arrived(swap)
 
     def other_squares(i, carry):
@@ -257,6 +253,8 @@
 
     lax.fori_loop(0, 4, other_squares, 0)
     arrived(batch_p)
+    arrived(nys_z)
+    nys_own = links.start([(nys(blocks[0], 256), nys(blocks[0], 256), links.core())])
     piece = [nys(blocks[0] + 128 * i, 128) for i in range(2)]
     nys_p = links.start([(piece[0], piece[0], links.along_p(k)) for k in (1, 3)])
 
@@ -309,7 +307,7 @@
             )
 
     theirs = [(1 - c) * 1024 + ((q + k) % 4) * 256 for k in range(4)]
-    here = at(2048 + c * 256, 256)
+    here = at(c * 256, 256)
 
     def start_sum_q(h):
         arrived(sum_p[h])
@@ -355,7 +353,7 @@
         return links.start([(tile, tile, links.along_z(k)) for k in range(1, 8)])
 
     def resid_rows(h, first, count):
-        return coefs.at[at(512 * h + first, count), here]
+        return resid.at[at(512 * h + first, count), here]
 
     def start_resid_q(h):
         arrived(resid_z[h])
@@ -453,42 +451,40 @@
     high, middle, low = three(jnp.where(narrow, value * wide_corr[:, 128:256], 0.0))
     mixed[rows, 384:512] = beside(high, middle, low)
     mixed_core = links.start([(mixed.at[rows, :], mixed.at[rows, :], links.core())])
-    narrow = lax.broadcasted_iota(jnp.int32, (512, 128), 1) < 32
-
-    def project(h):
-        rows = slice(512 * h, 512 * h + 512)
-        value = jnp.dot(coefs[rows, 2048:2560], mixed[...], preferred_element_type=F32)
-        high, middle, _ = three(value[:, 0:128] + value[:, 128:256] + value[:, 256:384])
-        scaled[rows, 0:128] = high
-        scaled[rows, 128:256] = middle
-        scaled[rows, 256:384] = high
-        value = value[:, 384:512]
-        value = value + pltpu.roll(value, 96, 1) + pltpu.roll(value, 64, 1)
-        high, middle, _ = three(jnp.where(narrow, value, 0.0))
-        scaled[rows, 384:512] = beside(high, middle, high)
-
-    def finish(h):
-        rows = slice(512 * h, 512 * h + 512)
-        for i in range(4):
-            cols = slice(512 * i, 512 * i + 512)
-            coefs[rows, cols] = (-by_rows(scaled[rows, :], stack[cols, 0:512])).astype(BF16)
-        kept = min(512, OUT - 512 * h)
-        for i in range(4):
-            cols = slice(256 * i, 256 * i + 256)
-            change = by_rows(coefs[rows, :], table[cols, :])
-            out[512 * h : 512 * h + kept, cols] = (RATE / BATCH) * change[0:kept]
-
-    resid_core = pass_on(0)
+    resid_core = pass_on(0) + pass_on(1)
     arrived(mixed_core)
     arrived(resid_core)
-    project(0)
-    resid_core = pass_on(1)
-    finish(0)
-    arrived(resid_core)
-    project(1)
-    finish(1)
     for copy in links.all:
         copy.wait_send()
+
+
+def tail_kernel(old, stack, table, mixed, resid, out, scaled, coefs, new, sent):
+    narrow = lax.broadcasted_iota(jnp.int32, (1024, 128), 1) < 32
+    value = jnp.dot(resid[...], mixed[...], preferred_element_type=F32)
+    high, middle, _ = three(value[:, 0:128] + value[:, 128:256] + value[:, 256:384])
+    scaled[:, 0:128] = high
+    scaled[:, 128:256] = middle
+    scaled[:, 256:384] = high
+    value = value[:, 384:512]
+    value = value + pltpu.roll(value, 96, 1) + pltpu.roll(value, 64, 1)
+    high, middle, _ = three(jnp.where(narrow, value, 0.0))
+    scaled[:, 384:512] = beside(high, middle, high)
+    for i in range(4):
+        cols = slice(512 * i, 512 * i + 512)
+        for k in range(2):
+            rows = slice(512 * k, 512 * k + 512)
+            coefs[rows, cols] = (-by_rows(scaled[rows, :], stack[cols, 0:512])).astype(BF16)
+    coefs[:, NYS : NYS + BATCH] = resid[...]
+    copies = []
+    for i in range(4):
+        cols = slice(256 * i, 256 * i + 256)
+        for rows in (slice(0, 512), slice(512, OUT)):
+            change = by_rows(coefs[rows.start : rows.start + 512, :], table[cols, :])
+            new[rows, cols] = old[rows, cols] - (RATE / BATCH) * change[0 : rows.stop - rows.start]
+        copies.append(pltpu.make_async_copy(new.at[:, cols], out.at[:, cols], sent.at[i]))
+        copies[-1].start()
+    for copy in copies:
+        copy.wait()
 
 
 def by_rows(a, b):
@@ -503,11 +499,17 @@
 def per_device(centers, weights, batch_points, labels, nystrom_points, eigvecs, corrections):
     hbm = pl.BlockSpec(memory_space=pltpu.HBM)
     vmem = pltpu.VMEM
-    change = pl.pallas_call(
+    inner = pl.BlockSpec(memory_space=vmem)
+    handed = pl.pallas_call(
         step_kernel,
-        out_shape=jax.ShapeDtypeStruct((OUT, CEN), F32),
+        out_shape=(
+            jax.ShapeDtypeStruct((NYS, 768), BF16),
+            jax.ShapeDtypeStruct((1280, NYS + BATCH), BF16),
+            jax.ShapeDtypeStruct((BATCH, 512), BF16),
+            jax.ShapeDtypeStruct((1024, BATCH), BF16),
+        ),
         in_specs=[hbm] * 7,
-        out_specs=pl.BlockSpec(memory_space=vmem),
+        out_specs=(inner,) * 4,
         scratch_shapes=[
             vmem((2304, FEATURES), BF16),
             vmem((1280, 1), F32),
@@ -525,7 +527,6 @@
             vmem((OUT, CEN), F32),
             vmem((1024, 2048), BF16),
             vmem((64, 40, 128), F32),
-            vmem((NYS, 768), BF16),
             vmem((256, 2048), BF16),
             vmem((1024, 256), F32),
             vmem((1024, 256), F32),
@@ -535,16 +536,12 @@
             vmem((2, 3, 32, 256), F32),
             vmem((2, 7, 8, 128), F32),
             vmem((2, 8, 8, 128), F32),
-            vmem((1280, 2560), BF16),
-            vmem((BATCH, 512), BF16),
-            vmem((1024, 2560), BF16),
-            vmem((1024, 512), BF16),
             pltpu.SemaphoreType.DMA((110,)),
             pltpu.SemaphoreType.DMA((110,)),
             pltpu.SemaphoreType.DMA((7,)),
         ],
         compiler_params=pltpu.CompilerParams(
-            collective_id=0, has_side_effects=True, vmem_limit_bytes=50 << 20
+            collective_id=0, has_side_effects=True, vmem_limit_bytes=38 << 20
         ),
         name="step",
     )(
@@ -561,7 +558,20 @@
             )
         )
     )
-    return (weights.T - change).T
+    return pl.pallas_call(
+        tail_kernel,
+        out_shape=jax.ShapeDtypeStruct((OUT, CEN), F32),
+        in_specs=[inner] * 5,
+        out_specs=hbm,
+        scratch_shapes=[
+            vmem((1024, 512), BF16),
+            vmem((1024, NYS + BATCH), BF16),
+            vmem((OUT, CEN), F32),
+            pltpu.SemaphoreType.DMA((4,)),
+        ],
+        compiler_params=pltpu.CompilerParams(vmem_limit_bytes=24 << 20),
+        name="tail",
+    )(weights.T, *handed).T
 
 
 def solution(mesh):

time: 78.1 us -> 80.7 us (1.033)
  Pallas kernels: 74.7 us -> 80.5 us
  other arithmetic: 3.31 us -> 0 us
    pallas_call x1 -> x2, Pallas kernels: 74.7 us -> 80.5 us  [the longest x1 71.1 us: per_device(): pl.pallas_call(step_kernel, out_shape=(jax.ShapeDtypeStruct((NYS, 768), B...]
    transpose x1 -> x0, other arithmetic: 3.31 us -> none  [per_device(): return (weights.T - change).T]
where the time goes in v5:
time: 80.7 us
  Pallas kernels  80.5 us (100%)
    pallas_call x1, Pallas kernels, per_device(): pl.pallas_call(step_kernel, out_shape=(jax.ShapeDtypeStruct((NYS, 768), B...  71.1 us
    pallas_call x1, Pallas kernels, per_device(): pl.pallas_call(tail_kernel, out_shape=jax.ShapeDtypeStruct((OUT, CEN), F3...  9.37 us

profile of v5, /device:TPU:1, one launch (start us, length us, event | category | flops | bytes accessed | tf_op | source)
XLA Modules:
  0.0 80.7 jit_solution(4516875717845192049)
XLA Ops:
  0.0 0.0 copy-start
  0.0 71.1 %step.1 = (bf16[2048,768]{1,0:T(8,128)(2,1)S(1)}, bf16[1280,2560]{1,0:T(8,128)(2,1)S(1)}, bf16[512,512]{1,0:T(8,128)(2,1)S(1)}, bf16[1024,512]{1,0:T(8,128)(2,1)S(1)}) custom-call(bf16[1024,1024]{1,0:T(8,128)(2,1)} %centers.1, f32[1000,1024]{1,0:T(8,128)} %bitcast.3, bf16[2,1024]{1,0:T(2,128)(2,1)} %batch.1, f32[2,1000]{1,0:T(2,128)} %labels.1, ...), custom_call_target="tpu_custom_call" | custom-call | tf_op jit(solution)/shard_map/step/pallas_call | solution.py:503
  71.1 0.0 copy-done
  71.1 9.4 %tail.1 = f32[1000,1024]{1,0:T(8,128)} custom-call(f32[1000,1024]{1,0:T(8,128)S(1)} %bitcast.4, bf16[2048,768]{1,0:T(8,128)(2,1)S(1)} %get-tuple-element.9.stack, bf16[1280,2560]{1,0:T(8,128)(2,1)S(1)} %get-tuple-element.10.table, bf16[512,512]{1,0:T(8,128)(2,1)S(1)} %get-tuple-element.11.mixed, bf16[1024,512]{1,0:T(8,128)(2,1)S(1)} %get-tuple-element.12.resid), custom_call_target="tpu_custom_call" | custom-call | tf_op jit(solution)/shard_map/tail/pallas_call | solution.py:561
Async XLA Ops:
  0.0 71.1 %copy-start = (f32[1024,1000]{0,1:T(8,128)S(1)}, f32[1024,1000]{0,1:T(8,128)}, u32[]{:S(2)}) copy-start(f32[1024,1000]{0,1:T(8,128)} %param.8) | copy-start | bytes 12288004

commit v6 on v5

--- a/solution.py
+++ b/solution.py
@@ -123,6 +123,7 @@
     table,
     mixed,
     resid,
+    coefs,
     left,
     left_sq,
     right,
@@ -148,6 +149,7 @@
     from_q,
     from_z,
     gathered,
+    scaled,
     send,
     recv,
     local,
@@ -156,7 +158,7 @@
     c, p, q, z = links.c, links.p, links.q, links.z
     group = p * 4 + q
 
-    own_n = c * 1024 + p * 256 + (z % 2) * 128 + q * 32
+    own_n = c * 1024 + p * 256 + q * 64 + (z % 2) * 32
     loads = [
         (batch, small_batch),
         (labels, small_labels),
@@ -196,19 +198,19 @@
         return eig.at[pl.ds(first // 32, count // 32)]
 
     tile = tiles.at[at(group * 16, 16), at(z * 128, 128)]
-    batch_z = links.start([(tile, tile, links.along_z(k)) for k in range(1, 8)])
+    batch_q = links.start([(tile, tile, links.along_q(k)) for k in range(1, 4)])
     own = [nys(own_n, 32), vectors(own_n, 32)]
-    nys_q = links.start([(o, o, links.along_q(k)) for k in range(1, 4) for o in own])
+    nys_z = links.start([(o, o, links.z_pair()) for o in own])
     loads[4].wait()
     swap = links.start([(left.at[0:1024, :], left.at[1280:2304, :], links.core())])
 
-    arrived(batch_z)
-    tile = tiles.at[at(group * 16, 16), :]
-    batch_q = links.start([(tile, tile, links.along_q(k)) for k in range(1, 4)])
-    arrived(nys_q)
-    own_z = c * 1024 + p * 256 + (z % 2) * 128
-    own = [nys(own_z, 128), vectors(own_z, 128)]
-    nys_z = links.start([(o, o, links.z_pair()) for o in own])
+    arrived(batch_q)
+    tile = tiles.at[at(p * 64, 64), at(z * 128, 128)]
+    batch_z = links.start([(tile, tile, links.along_z(k)) for k in range(1, 8)])
+    arrived(nys_z)
+    own_q = c * 1024 + p * 256 + q * 64
+    own = [nys(own_q, 64), vectors(own_q, 64)]
+    nys_q = links.start([(o, o, links.along_q(k)) for k in range(1, 4) for o in own])
 
     loads[5].wait()
     for i in range(7):
@@ -218,7 +220,7 @@
     rounded[896:1024, 0:1024] = last.astype(BF16)
     swap += links.start([(rounded.at[:, 0:1024], rounded.at[:, 1024:2048], links.core())])
 
-    arrived(batch_q)
+    arrived(batch_z)
     block = tiles.at[at(p * 64, 64), :]
     batch_p = links.start([(block, block, links.along_p(k)) for k in range(1, 4)])
 
@@ -241,7 +243,9 @@
             lane == point, wide_labels[0], jnp.where(lane == point + 8, wide_labels[1], 0.0)
         )
     placed[OUT:1024, :] = jnp.zeros((1024 - OUT, 256), F32)
+    arrived(nys_q)
     blocks = [c * 1024 + ((p + k) % 4) * 256 for k in range(4)]
+    nys_own = links.start([(nys(blocks[0], 256), nys(blocks[0], 256), links.core())])
     arrived(swap)
 
     def other_squares(i, carry):
@@ -253,8 +257,6 @@
 
     lax.fori_loop(0, 4, other_squares, 0)
     arrived(batch_p)
-    arrived(nys_z)
-    nys_own = links.start([(nys(blocks[0], 256), nys(blocks[0], 256), links.core())])
     piece = [nys(blocks[0] + 128 * i, 128) for i in range(2)]
     nys_p = links.start([(piece[0], piece[0], links.along_p(k)) for k in (1, 3)])
 
@@ -451,16 +453,20 @@
     high, middle, low = three(jnp.where(narrow, value * wide_corr[:, 128:256], 0.0))
     mixed[rows, 384:512] = beside(high, middle, low)
     mixed_core = links.start([(mixed.at[rows, :], mixed.at[rows, :], links.core())])
-    resid_core = pass_on(0) + pass_on(1)
+    resid_core = pass_on(0)
     arrived(mixed_core)
+    arrived(resid_core)
+    project(resid[0:512, :], mixed, scaled)
+    resid_core = pass_on(1)
+    correct(scaled, stack, coefs)
     arrived(resid_core)
     for copy in links.all:
         copy.wait_send()
 
 
-def tail_kernel(old, stack, table, mixed, resid, out, scaled, coefs, new, sent):
-    narrow = lax.broadcasted_iota(jnp.int32, (1024, 128), 1) < 32
-    value = jnp.dot(resid[...], mixed[...], preferred_element_type=F32)
+def project(resid, mixed, scaled):
+    narrow = lax.broadcasted_iota(jnp.int32, (512, 128), 1) < 32
+    value = jnp.dot(resid, mixed[...], preferred_element_type=F32)
     high, middle, _ = three(value[:, 0:128] + value[:, 128:256] + value[:, 256:384])
     scaled[:, 0:128] = high
     scaled[:, 128:256] = middle
@@ -469,11 +475,18 @@
     value = value + pltpu.roll(value, 96, 1) + pltpu.roll(value, 64, 1)
     high, middle, _ = three(jnp.where(narrow, value, 0.0))
     scaled[:, 384:512] = beside(high, middle, high)
+
+
+def correct(scaled, stack, coefs):
     for i in range(4):
         cols = slice(512 * i, 512 * i + 512)
-        for k in range(2):
-            rows = slice(512 * k, 512 * k + 512)
-            coefs[rows, cols] = (-by_rows(scaled[rows, :], stack[cols, 0:512])).astype(BF16)
+        coefs[:, cols] = (-by_rows(scaled[...], stack[cols, 0:512])).astype(BF16)
+
+
+def tail_kernel(old, stack, table, mixed, resid, first, out, scaled, coefs, new, sent):
+    coefs[0:512, 0:NYS] = first[...]
+    project(resid[512:1024, :], mixed, scaled)
+    correct(scaled, stack, coefs.at[512:1024, :])
     coefs[:, NYS : NYS + BATCH] = resid[...]
     copies = []
     for i in range(4):
@@ -507,9 +520,10 @@
             jax.ShapeDtypeStruct((1280, NYS + BATCH), BF16),
             jax.ShapeDtypeStruct((BATCH, 512), BF16),
             jax.ShapeDtypeStruct((1024, BATCH), BF16),
+            jax.ShapeDtypeStruct((512, NYS), BF16),
         ),
         in_specs=[hbm] * 7,
-        out_specs=(inner,) * 4,
+        out_specs=(inner,) * 5,
         scratch_shapes=[
             vmem((2304, FEATURES), BF16),
             vmem((1280, 1), F32),
@@ -536,6 +550,7 @@
             vmem((2, 3, 32, 256), F32),
             vmem((2, 7, 8, 128), F32),
             vmem((2, 8, 8, 128), F32),
+            vmem((512, 512), BF16),
             pltpu.SemaphoreType.DMA((110,)),
             pltpu.SemaphoreType.DMA((110,)),
             pltpu.SemaphoreType.DMA((7,)),
@@ -561,10 +576,10 @@
     return pl.pallas_call(
         tail_kernel,
         out_shape=jax.ShapeDtypeStruct((OUT, CEN), F32),
-        in_specs=[inner] * 5,
+        in_specs=[inner] * 6,
         out_specs=hbm,
         scratch_shapes=[
-            vmem((1024, 512), BF16),
+            vmem((512, 512), BF16),
             vmem((1024, NYS + BATCH), BF16),
             vmem((OUT, CEN), F32),
             pltpu.SemaphoreType.DMA((4,)),

time: 80.7 us -> 76 us (0.942)
  Pallas kernels: 80.5 us -> 75.7 us
    pallas_call x1, Pallas kernels: 71.1 us -> 67.6 us  [per_device(): pl.pallas_call(step_kernel, out_shape=(jax.ShapeDtypeStruct((NYS, 768), B...]
    pallas_call x1, Pallas kernels: 9.37 us -> 8.11 us  [per_device(): pl.pallas_call(tail_kernel, out_shape=jax.ShapeDtypeStruct((OUT, CEN), F3...]
where the time goes in v6:
time: 76 us; the launch traced here: 75.9 us
  Pallas kernels  75.7 us (100%)
    pallas_call x1, Pallas kernels, per_device(): pl.pallas_call(step_kernel, out_shape=(jax.ShapeDtypeStruct((NYS, 768), B...  67.6 us
    pallas_call x1, Pallas kernels, per_device(): pl.pallas_call(tail_kernel, out_shape=jax.ShapeDtypeStruct((OUT, CEN), F3...  8.11 us

profile of v6, /device:TPU:1, one launch (start us, length us, event | category | flops | bytes accessed | tf_op | source)
XLA Modules:
  0.0 75.9 jit_solution(844361635480320865)
XLA Ops:
  0.0 0.0 copy-start
  0.0 67.6 %step.1 = (bf16[2048,768]{1,0:T(8,128)(2,1)S(1)}, bf16[1280,2560]{1,0:T(8,128)(2,1)S(1)}, bf16[512,512]{1,0:T(8,128)(2,1)S(1)}, bf16[1024,512]{1,0:T(8,128)(2,1)S(1)}, bf16[512,2048]{1,0:T(8,128)(2,1)S(1)}) custom-call(bf16[1024,1024]{1,0:T(8,128)(2,1)} %centers.1, f32[1000,1024]{1,0:T(8,128)} %bitcast.3, bf16[2,1024]{1,0:T(2,128)(2,1)} %batch.1, ...), custom_call_target="tpu_custom_call" | custom-call | tf_op jit(solution)/shard_map/step/pallas_call | solution.py:516
  67.6 0.0 copy-done
  67.6 8.1 %tail.1 = f32[1000,1024]{1,0:T(8,128)} custom-call(f32[1000,1024]{1,0:T(8,128)S(1)} %bitcast.4, bf16[2048,768]{1,0:T(8,128)(2,1)S(1)} %get-tuple-element.10.stack, bf16[1280,2560]{1,0:T(8,128)(2,1)S(1)} %get-tuple-element.11.table, bf16[512,512]{1,0:T(8,128)(2,1)S(1)} %get-tuple-element.12.mixed, bf16[1024,512]{1,0:T(8,128)(2,1)S(1)} %get-tuple-element.13.resid, ...), custom_call_target="tpu_custom_call" | custom-call | tf_op jit(solution)/shard_map/tail/pallas_call | solution.py:576
Async XLA Ops:
  0.0 67.6 %copy-start = (f32[1024,1000]{0,1:T(8,128)S(1)}, f32[1024,1000]{0,1:T(8,128)}, u32[]{:S(2)}) copy-start(f32[1024,1000]{0,1:T(8,128)} %param.8) | copy-start | bytes 12288004

commit v7 on v6

--- a/solution.py
+++ b/solution.py
@@ -299,11 +299,13 @@
     right[own_b, :] = left[1024:1280, :]
     batch_own = links.start([(right.at[own_b, :], right.at[own_b, :], links.core())])
 
-    def fill(first, height):
+    def fill(first, end, begin=0, norms=True):
         cols = pl.ds(pl.multiple_of(first, 256), 256)
-        right_sq[:, cols] = as_row(square_sums(right[cols, :]))
-        for i in range(2):
-            rows = slice(i * (height // 2), (i + 1) * (height // 2))
+        if norms:
+            right_sq[:, cols] = as_row(square_sums(right[cols, :]))
+        count = max((end - begin) // 2, 256)
+        for i in range(begin, end, count):
+            rows = slice(i, i + count)
             table[rows, cols] = kernel_values(
                 left[rows, :], left_sq[rows, :], right[cols, :], right_sq[:, cols]
             )
@@ -383,8 +385,8 @@
     fill(blocks[0], 1280)
     arrived(nys_own)
     fill(theirs[0], 1280)
+    fill(2048 + c * 256, 1024)
     sum_q = [start_sum_q(0)]
-    fill(2048 + c * 256, 1024)
     sum_q.append(start_sum_q(1))
     nys_p += links.start([(piece[1], piece[1], links.along_p(k)) for k in (1, 3)])
     mine = vectors(blocks[0], 256)
@@ -404,18 +406,14 @@
     fill(blocks[3], 1280)
     arrived(nys_core)
     fill(theirs[1], 1280)
-    fill(theirs[3], 1280)
     resid_q = [start_resid_q(0)]
     resid_q.append(start_resid_q(1))
     arrived(eig_p)
     eig_core = links.start([(vectors(c * 1024, 1024), vectors(c * 1024, 1024), links.core())])
     arrived(nys_far)
     nys_last = links.start([(nys(blocks[2], 256), nys(blocks[2], 256), links.core())])
-    fill(blocks[2], 1280)
-    resid_p = [start_resid_p(0)]
-    resid_p.append(start_resid_p(1))
-    arrived(eig_core)
-
+    fill(theirs[3], 1280)
+    fill(blocks[2], 1280, 1024)
     narrow = lax.broadcasted_iota(jnp.int32, (256, 128), 1) < 32
 
     def split(i, carry):
@@ -434,9 +432,13 @@
         stack[rows, 640:768] = low
         return carry
 
-    lax.fori_loop(0, 8, split, 0)
+    lax.fori_loop(c * 4, c * 4 + 4, split, 0)
+    resid_p = [start_resid_p(0)]
+    resid_p.append(start_resid_p(1))
+    arrived(eig_core)
+    lax.fori_loop(4 - c * 4, 8 - c * 4, split, 0)
     arrived(nys_last)
-    fill(theirs[2], 1280)
+    fill(theirs[2], 1280, 1024)
 
     loads[6].wait()
     wide_corr[...] = jnp.zeros((1, 256), F32)
@@ -453,6 +455,8 @@
     high, middle, low = three(jnp.where(narrow, value * wide_corr[:, 128:256], 0.0))
     mixed[rows, 384:512] = beside(high, middle, low)
     mixed_core = links.start([(mixed.at[rows, :], mixed.at[rows, :], links.core())])
+    fill(blocks[2], 1024, norms=False)
+    fill(theirs[2], 1024, norms=False)
     resid_core = pass_on(0)
     arrived(mixed_core)
     arrived(resid_core)

time: 76 us -> 75 us (0.987)
  Pallas kernels: 75.7 us -> 74.7 us
    pallas_call x1, Pallas kernels: 67.6 us -> 66.6 us  [per_device(): pl.pallas_call(step_kernel, out_shape=(jax.ShapeDtypeStruct((NYS, 768), B...]
where the time goes in v7:
time: 75 us; the launch traced here: 74.9 us
  Pallas kernels  74.7 us (100%)
    pallas_call x1, Pallas kernels, per_device(): pl.pallas_call(step_kernel, out_shape=(jax.ShapeDtypeStruct((NYS, 768), B...  66.6 us
    pallas_call x1, Pallas kernels, per_device(): pl.pallas_call(tail_kernel, out_shape=jax.ShapeDtypeStruct((OUT, CEN), F3...  8.11 us

profile of v7, /device:TPU:1, one launch (start us, length us, event | category | flops | bytes accessed | tf_op | source)
XLA Modules:
  0.0 74.9 jit_solution(13091441415268863975)
XLA Ops:
  0.0 0.0 copy-start
  0.0 66.6 %step.1 = (bf16[2048,768]{1,0:T(8,128)(2,1)S(1)}, bf16[1280,2560]{1,0:T(8,128)(2,1)S(1)}, bf16[512,512]{1,0:T(8,128)(2,1)S(1)}, bf16[1024,512]{1,0:T(8,128)(2,1)S(1)}, bf16[512,2048]{1,0:T(8,128)(2,1)S(1)}) custom-call(bf16[1024,1024]{1,0:T(8,128)(2,1)} %centers.1, f32[1000,1024]{1,0:T(8,128)} %bitcast.3, bf16[2,1024]{1,0:T(2,128)(2,1)} %batch.1, ...), custom_call_target="tpu_custom_call" | custom-call | tf_op jit(solution)/shard_map/step/pallas_call | solution.py:520
  66.6 0.0 copy-done
  66.6 8.1 %tail.1 = f32[1000,1024]{1,0:T(8,128)} custom-call(f32[1000,1024]{1,0:T(8,128)S(1)} %bitcast.4, bf16[2048,768]{1,0:T(8,128)(2,1)S(1)} %get-tuple-element.10.stack, bf16[1280,2560]{1,0:T(8,128)(2,1)S(1)} %get-tuple-element.11.table, bf16[512,512]{1,0:T(8,128)(2,1)S(1)} %get-tuple-element.12.mixed, bf16[1024,512]{1,0:T(8,128)(2,1)S(1)} %get-tuple-element.13.resid, ...), custom_call_target="tpu_custom_call" | custom-call | tf_op jit(solution)/shard_map/tail/pallas_call | solution.py:580
Async XLA Ops:
  0.0 66.6 %copy-start = (f32[1024,1000]{0,1:T(8,128)S(1)}, f32[1024,1000]{0,1:T(8,128)}, u32[]{:S(2)}) copy-start(f32[1024,1000]{0,1:T(8,128)} %param.8) | copy-start | bytes 12288004

commit v8 on v7

--- a/solution.py
+++ b/solution.py
@@ -347,23 +347,26 @@
             ]
         )
 
-    def start_resid_z(h):
-        arrived(sum_z[h])
-        total = share(h, z)[...]
-        for k in range(7):
-            total = total + from_z[h, k]
-        gathered[h, z] = total
-        tile = gathered.at[h, z]
+    def start_resid_z():
+        totals = []
+        for h in range(2):
+            arrived(sum_z[h])
+            total = share(h, z)[...]
+            for k in range(7):
+                total = total + from_z[h, k]
+            totals.append(total)
+        gathered[z] = jnp.concatenate(totals, axis=0).astype(BF16)
+        tile = gathered.at[z]
         return links.start([(tile, tile, links.along_z(k)) for k in range(1, 8)])
 
     def resid_rows(h, first, count):
         return resid.at[at(512 * h + first, count), here]
 
     def start_resid_q(h):
-        arrived(resid_z[h])
-        rows = [
-            jnp.concatenate([gathered[h, 2 * i], gathered[h, 2 * i + 1]], axis=1) for i in range(4)
-        ]
+        rows = []
+        for i in range(0, 8, 2):
+            pair = [gathered[i + m].astype(F32)[8 * h : 8 * h + 8] for m in range(2)]
+            rows.append(jnp.concatenate(pair, axis=1))
         tile = resid_rows(h, p * 128 + q * 32, 32)
         tile[...] = jnp.concatenate(rows, axis=0).astype(BF16)
         return links.start([(tile, tile, links.along_q(k)) for k in range(1, 4)])
@@ -396,8 +399,7 @@
     sum_z = [start_sum_z(0)]
     sum_z.append(start_sum_z(1))
     nys_far = links.start([(nys(blocks[0], 256), nys(blocks[0], 256), links.along_p(2))])
-    resid_z = [start_resid_z(0)]
-    resid_z.append(start_resid_z(1))
+    resid_z = start_resid_z()
     arrived(nys_p)
     nys_core = links.start(
         [(nys(blocks[k], 256), nys(blocks[k], 256), links.core()) for k in (1, 3)]
@@ -406,6 +408,7 @@
     fill(blocks[3], 1280)
     arrived(nys_core)
     fill(theirs[1], 1280)
+    arrived(resid_z)
     resid_q = [start_resid_q(0)]
     resid_q.append(start_resid_q(1))
     arrived(eig_p)
@@ -553,7 +556,7 @@
             vmem((2, 3, 128, 256), F32),
             vmem((2, 3, 32, 256), F32),
             vmem((2, 7, 8, 128), F32),
-            vmem((2, 8, 8, 128), F32),
+            vmem((8, 16, 128), BF16),
             vmem((512, 512), BF16),
             pltpu.SemaphoreType.DMA((110,)),
             pltpu.SemaphoreType.DMA((110,)),

time: 75 us -> 75.1 us (level)
  no operation moved by 1% of the time
where the time goes in v8:
time: 75.1 us; the launch traced here: 75 us
  Pallas kernels  74.9 us (100%)
    pallas_call x1, Pallas kernels, per_device(): pl.pallas_call(step_kernel, out_shape=(jax.ShapeDtypeStruct((NYS, 768), B...  66.7 us
    pallas_call x1, Pallas kernels, per_device(): pl.pallas_call(tail_kernel, out_shape=jax.ShapeDtypeStruct((OUT, CEN), F3...  8.11 us

profile of v8, /device:TPU:1, one launch (start us, length us, event | category | flops | bytes accessed | tf_op | source)
XLA Modules:
  0.0 75.0 jit_solution(18247734067358413399)
XLA Ops:
  0.0 0.0 copy-start
  0.0 66.7 %step.1 = (bf16[2048,768]{1,0:T(8,128)(2,1)S(1)}, bf16[1280,2560]{1,0:T(8,128)(2,1)S(1)}, bf16[512,512]{1,0:T(8,128)(2,1)S(1)}, bf16[1024,512]{1,0:T(8,128)(2,1)S(1)}, bf16[512,2048]{1,0:T(8,128)(2,1)S(1)}) custom-call(bf16[1024,1024]{1,0:T(8,128)(2,1)} %centers.1, f32[1000,1024]{1,0:T(8,128)} %bitcast.3, bf16[2,1024]{1,0:T(2,128)(2,1)} %batch.1, ...), custom_call_target="tpu_custom_call" | custom-call | tf_op jit(solution)/shard_map/step/pallas_call | solution.py:523
  66.8 0.0 copy-done
  66.8 8.1 %tail.1 = f32[1000,1024]{1,0:T(8,128)} custom-call(f32[1000,1024]{1,0:T(8,128)S(1)} %bitcast.4, bf16[2048,768]{1,0:T(8,128)(2,1)S(1)} %get-tuple-element.10.stack, bf16[1280,2560]{1,0:T(8,128)(2,1)S(1)} %get-tuple-element.11.table, bf16[512,512]{1,0:T(8,128)(2,1)S(1)} %get-tuple-element.12.mixed, bf16[1024,512]{1,0:T(8,128)(2,1)S(1)} %get-tuple-element.13.resid, ...), custom_call_target="tpu_custom_call" | custom-call | tf_op jit(solution)/shard_map/tail/pallas_call | solution.py:583
Async XLA Ops:
  0.0 66.8 %copy-start = (f32[1024,1000]{0,1:T(8,128)S(1)}, f32[1024,1000]{0,1:T(8,128)}, u32[]{:S(2)}) copy-start(f32[1024,1000]{0,1:T(8,128)} %param.8) | copy-start | bytes 12288004
